TPU v7x, 256 devices: a whole 4x4x8 slice. The times are simulated.
256 devices in a mesh: ctx: 16 (over x, y_hi, core), grp: 16 (over y_lo, z).
Axes of the slice: x: 4, y: 4 (y_hi: 2, y_lo: 2; y = y_hi * 2 + y_lo), z: 8, core: 2. Of those that a mesh axis runs over, the one named last changes fastest.
Arguments:
- tokens: bfloat16 [65536, 2560], P(('ctx', 'grp')), may hold values from -6 to 6
- norm_gain: bfloat16 [2560], replicated, may hold values from 0.5 to 1.5
- w_query: bfloat16 [2560, 2560], P('grp'), may hold values from -0.125 to 0.125
- w_key: bfloat16 [2560, 512], P('grp'), may hold values from -0.125 to 0.125
- w_value: bfloat16 [2560, 512], P('grp'), may hold values from -0.125 to 0.125
- b_query: bfloat16 [2560], replicated, may hold values from -3 to 3
- b_key: bfloat16 [512], replicated, may hold values from -3 to 3
- b_value: bfloat16 [512], replicated, may hold values from -3 to 3
- cache_keys: bfloat16 [2048, 512], P('ctx'), may hold values from -140 to 140
- cache_values: bfloat16 [2048, 512], P('ctx'), may hold values from -6 to 6
- block_lists: int32 [20, 512, 4], P(None, ('ctx', 'grp')), may hold values from -1 to 15, as said below
- start_position: int32 [1], replicated, may hold values from 0 to 983040
Outputs:
- context: float32 [65536, 2560], P(('ctx', 'grp'))
- keys_new: float32 [65536, 512], P(('ctx', 'grp'))
- values_new: float32 [65536, 512], P(('ctx', 'grp'))
Inputs may be any that keep to these rules, and one draw needn't show every extreme that they name: `block_lists`: each list names distinct blocks of 128 prefix positions, named blocks first and -1 in the empty slots after them; every list names at least one block, some list names 4 and some only one.
All inputs are finite; a program needn't handle non-finite values.
Results may differ from a plain program's by a relative error of at most 0.034.
Values may be sent and summed in bfloat16 or wider, within the bound.
A program may use at most 128 MiB of HBM per device.

v0:
```python
import jax
import jax.numpy as jnp
import numpy as np
from jax import lax
from jax.sharding import PartitionSpec as P

HD = 128
GROUP = 5
QBLK = 128


norm_eps = 1e-06
rope_base = 10000000.0


def angle_tables(head_dim):
    half_dim = head_dim // 2
    frequency = rope_base ** (-2.0 * np.arange(half_dim) / head_dim)
    return np.stack(
        [np.mod(frequency * 32.0**digit_level, 2.0 * np.pi) for digit_level in range(4)]
    )


def rotate(values, positions):
    head_dim = values.shape[-1]
    half_dim = head_dim // 2
    tables = jnp.asarray(angle_tables(head_dim), jnp.float32)
    angles = jnp.zeros((positions.shape[0], half_dim), jnp.float32)
    remaining = positions
    for digit_level in range(4):
        digit_value = (remaining % 32).astype(jnp.float32)
        angles = angles + digit_value[:, None] * tables[digit_level][None, :]
        remaining = remaining // 32
    cosine = jnp.cos(angles)[:, None, :]
    sine_part = jnp.sin(angles)[:, None, :]
    lower_half = values[..., :half_dim]
    upper_half = values[..., half_dim:]
    return jnp.concatenate(
        [
            lower_half * cosine - upper_half * sine_part,
            upper_half * cosine + lower_half * sine_part,
        ],
        axis=-1,
    )


def on_device(
    tokens,
    norm_gain,
    w_query,
    w_key,
    w_value,
    b_query,
    b_key,
    b_value,
    cache_keys,
    cache_values,
    block_lists,
    start_position,
):
    row_count = tokens.shape[0]
    query_width = w_query.shape[1]
    kv_width = w_key.shape[1]
    heads_kv = kv_width // HD
    block_count = row_count // QBLK
    widened = tokens.astype(jnp.float32)
    normed = (
        widened
        * lax.rsqrt(jnp.mean(widened * widened, axis=-1, keepdims=True) + norm_eps)
        * norm_gain.astype(jnp.float32)
    ).astype(jnp.bfloat16)
    panels = (
        lax.all_gather(w_query, "grp", axis=0, tiled=True),
        lax.all_gather(w_key, "grp", axis=0, tiled=True),
        lax.all_gather(w_value, "grp", axis=0, tiled=True),
    )
    query_lin, key_lin, value_lin = tuple(
        (jnp.dot(normed, panel, preferred_element_type=jnp.float32) for panel in panels)
    )
    row_start = (lax.axis_index("ctx") * lax.axis_size("grp") + lax.axis_index("grp")) * row_count
    positions = start_position[0] + row_start + jnp.arange(row_count, dtype=jnp.int32)
    query = rotate(
        (query_lin + b_query.astype(jnp.float32)).reshape(row_count, heads_kv * GROUP, HD),
        positions,
    )
    keys_new = rotate(
        (key_lin + b_key.astype(jnp.float32)).reshape(row_count, heads_kv, HD), positions
    ).reshape(row_count, kv_width)
    values_new = value_lin + b_value.astype(jnp.float32)
    score_scale = HD ** (-0.5)
    query_heads = query.reshape(row_count, heads_kv, GROUP, HD)
    query_blocks = query.reshape(block_count, QBLK, heads_kv, GROUP, HD)
    key_blocks = keys_new.reshape(block_count, QBLK, heads_kv, HD)
    value_blocks = values_new.reshape(block_count, QBLK, heads_kv, HD)
    near_scores = jnp.einsum("bqkgd,bskd->kgbqs", query_blocks, key_blocks) * score_scale
    causal = lax.broadcasted_iota(jnp.int32, (QBLK, QBLK), 0) >= lax.broadcasted_iota(
        jnp.int32, (QBLK, QBLK), 1
    )
    near_scores = jnp.where(causal, near_scores, -jnp.inf)
    near_max = jnp.max(near_scores, axis=-1)
    near_exp = jnp.exp(near_scores - near_max[..., None])
    near_total = jnp.sum(near_exp, axis=-1)
    near_weighted = jnp.einsum("kgbqs,bskd->kgbqd", near_exp, value_blocks)
    initial_state = (
        near_max.reshape(heads_kv, GROUP, row_count),
        near_total.reshape(heads_kv, GROUP, row_count),
        near_weighted.reshape(heads_kv, GROUP, row_count, HD),
    )
    piece_keys = lax.all_gather(cache_keys, "ctx", axis=0, tiled=True)
    piece_values = lax.all_gather(cache_values, "ctx", axis=0, tiled=True)
    key_count = piece_keys.shape[0]

    def one_key_block(block_step, state_inner):
        old_max, old_total, old_weighted = state_inner
        block_keys = (
            lax.dynamic_slice_in_dim(piece_keys, block_step * QBLK, QBLK, 0)
            .reshape(QBLK, heads_kv, HD)
            .astype(jnp.float32)
        )
        block_values = (
            lax.dynamic_slice_in_dim(piece_values, block_step * QBLK, QBLK, 0)
            .reshape(QBLK, heads_kv, HD)
            .astype(jnp.float32)
        )
        attention_affinity = jnp.einsum("rkgd,pkd->kgrp", query_heads, block_keys) * score_scale
        listed = jnp.any(block_lists == block_step, axis=2).reshape(
            heads_kv, GROUP, block_count, 1, 1
        )
        attention_affinity = jnp.where(
            listed, attention_affinity.reshape(heads_kv, GROUP, block_count, QBLK, QBLK), -jnp.inf
        ).reshape(heads_kv, GROUP, row_count, QBLK)
        new_max = jnp.maximum(old_max, jnp.max(attention_affinity, axis=-1))
        factor = jnp.exp(old_max - new_max)
        weights = jnp.exp(attention_affinity - new_max[..., None])
        new_total = old_total * factor + jnp.sum(weights, axis=-1)
        new_weighted = old_weighted * factor[..., None] + jnp.einsum(
            "kgrp,pkd->kgrd", weights, block_values
        )
        return (new_max, new_total, new_weighted)

    final_max, row_total, weighted = lax.fori_loop(
        0, key_count // QBLK, one_key_block, initial_state
    )
    context = jnp.transpose(weighted / row_total[..., None], (2, 0, 1, 3)).reshape(
        row_count, query_width
    )
    return (context, keys_new, values_new)


def solution(mesh):
    in_specs = (
        P(("ctx", "grp"), None),
        P(),
        P("grp", None),
        P("grp", None),
        P("grp", None),
        P(),
        P(),
        P(),
        P("ctx", None),
        P("ctx", None),
        P(None, ("ctx", "grp"), None),
        P(),
    )
    out_specs = (P(("ctx", "grp"), None), P(("ctx", "grp"), None), P(("ctx", "grp"), None))
    return jax.shard_map(
        on_device, mesh=mesh, in_specs=in_specs, out_specs=out_specs, check_vma=False
    )
```

profile of v0, /device:TPU:1, one launch (start us, length us, event | category | flops | bytes accessed | tf_op | source)
XLA Modules:
  0.0 523.7 jit_solution(8601297681478014044)
XLA Ops:
  9.5 1.7 copy.59
  15.4 62.1 %all-gather.6.cloned.1.call-done = bf16[2560,512]{1,0:T(8,128)(2,1)} async-done(((bf16[160,512]{1,0:T(8,128)(2,1)}), bf16[2560,512]{1,0:T(8,128)(2,1)}) %all-gather.6.cloned.1.call-update) | async-done | bytes 2621456 | tf_op jit(solution)/shard_map/all_gather | solution.py:74
  77.5 2.6 convolution_add_fusion.2
  81.2 68.9 %all-gather.10.cloned.1.call-done = bf16[2560,512]{1,0:T(8,128)(2,1)} async-done(((bf16[160,512]{1,0:T(8,128)(2,1)}), bf16[2560,512]{1,0:T(8,128)(2,1)}) %all-gather.10.cloned.1.call-update) | async-done | bytes 2621456 | tf_op jit(solution)/shard_map/all_gather | solution.py:75
  150.2 2.6 convolution_add_fusion.1
  153.8 153.8 %all-gather.8.cloned.1.call-done = bf16[2560,2560]{1,0:T(8,128)(2,1)} async-done(((bf16[160,2560]{1,0:T(8,128)(2,1)}), bf16[2560,2560]{1,0:T(8,128)(2,1)}) %all-gather.8.cloned.1.call-update) | async-done | bytes 13107216 | tf_op jit(solution)/shard_map/all_gather | solution.py:73
  307.5 9.8 %convolution_add_fusion = f32[256,2560]{1,0:T(8,128)} fusion(bf16[2560,2560]{1,0:T(8,128)(2,1)} %all-gather.8.cloned.1.call-done, f32[2560]{0:T(1024)S(1)} %convert_element_type.64, bf16[256,2560]{1,0:T(8,128)(2,1)S(1)} %copy-done.2, f32[2560]{0:T(1024)S(1)} %convert_element_type.57, f32[256]{0:T(256)S(1)} %add_rsqrt_fusion), kind=kOutput, calls=%fused_computation.17 | convolution fusion | flops 3358720000 | bytes 17060864 | tf_op jit(solution)/shard_map/dot_general | solution.py:78
  317.4 2.1 copy.52
  324.0 2.4 copy.62
  326.5 2.3 fusion.15
  328.8 34.0 %all-gather.12.cloned.1.call-done = bf16[2048,512]{0,1:T(8,128)(2,1)} async-done(((bf16[128,512]{0,1:T(8,128)(2,1)}), bf16[2048,512]{0,1:T(8,128)(2,1)}) %all-gather.12.cloned.1.call-update) | async-done | bytes 2097168 | tf_op jit(solution)/shard_map/all_gather | solution.py:109
  362.8 55.9 %all-gather.14.cloned.1.call-done = bf16[2048,512]{0,1:T(8,128)(2,1)} async-done(((bf16[128,512]{0,1:T(8,128)(2,1)}), bf16[2048,512]{0,1:T(8,128)(2,1)}) %all-gather.14.cloned.1.call-update) | async-done | bytes 2097168 | tf_op jit(solution)/shard_map/all_gather | solution.py:110
  418.7 92.3 %while.17 = (s32[]{:T(128)}, f32[4,5,256]{2,1,0:T(8,128)S(1)}, f32[4,5,256]{2,1,0:T(8,128)S(1)}, f32[4,5,256,128]{3,2,1,0:T(8,128)S(1)}, s32[20,2,4]{0,2,1:T(4,1...) while((s32[]{:T(128)}, f32[4,5,256]{2,1,0:T(8,128)S(1)}, ...), condition=%wide.region_7.8_spmd, body=%wide.region_3.7_spmd.sunk | while | flops 343419168 | bytes 15574043 | solution.py:141
  420.0 1.9 fusion.51
  422.6 1.8 multiply_add_fusion.8
  425.8 1.9 fusion.51
  428.4 1.8 multiply_add_fusion.8
  431.6 1.9 fusion.51
  434.2 1.8 multiply_add_fusion.8
  437.4 1.9 fusion.51
  439.9 1.8 multiply_add_fusion.8
  443.1 1.9 fusion.51
  445.7 1.8 multiply_add_fusion.8
  448.9 1.9 fusion.51
  451.5 1.8 multiply_add_fusion.8
  454.7 1.9 fusion.51
  457.2 1.8 multiply_add_fusion.8
  460.4 1.9 fusion.51
  463.0 1.8 multiply_add_fusion.8
  466.2 1.9 fusion.51
  468.8 1.8 multiply_add_fusion.8
  472.0 1.9 fusion.51
  474.6 1.8 multiply_add_fusion.8
  477.7 1.9 fusion.51
  480.3 1.8 multiply_add_fusion.8
  483.5 1.9 fusion.51
  486.1 1.8 multiply_add_fusion.8
  489.3 1.9 fusion.51
  491.9 1.8 multiply_add_fusion.8
  495.1 1.9 fusion.51
  497.6 1.8 multiply_add_fusion.8
  500.8 1.9 fusion.51
  503.4 1.8 multiply_add_fusion.8
  506.6 1.9 fusion.51
  509.2 1.8 multiply_add_fusion.8
  511.0 2.1 copy.63
  513.1 2.0 broadcast_divide_fusion
  515.1 2.1 copy.64
  (235 shorter events, 44.2 us)
Async XLA Ops:
  7.2 7.5 %copy-start.8 = (f32[64]{0:T(128)S(1)}, f32[64]{0:T(128)}, u32[]{:S(2)}) copy-start(f32[64]{0:T(128)} %constant.155) | copy-start | bytes 772
  7.2 7.5 %copy-start.9 = (f32[64]{0:T(128)S(1)}, f32[64]{0:T(128)}, u32[]{:S(2)}) copy-start(f32[64]{0:T(128)} %constant.157) | copy-start | bytes 772
  7.2 7.5 %copy-start.10 = (f32[64]{0:T(128)S(1)}, f32[64]{0:T(128)}, u32[]{:S(2)}) copy-start(f32[64]{0:T(128)} %constant.159) | copy-start | bytes 772
  7.2 7.5 %copy-start.11 = (f32[64]{0:T(128)S(1)}, f32[64]{0:T(128)}, u32[]{:S(2)}) copy-start(f32[64]{0:T(128)} %constant.161) | copy-start | bytes 772
  7.2 7.1 %copy-start.2 = (bf16[256,2560]{1,0:T(8,128)(2,1)S(1)}, bf16[256,2560]{1,0:T(8,128)(2,1)}, u32[]{:S(2)}) copy-start(bf16[256,2560]{1,0:T(8,128)(2,1)} %param.16) | copy-start | bytes 3932164
  7.2 7.5 %copy-start.5 = (bf16[2560]{0:T(1024)(128)(2,1)S(1)}, bf16[2560]{0:T(1024)(128)(2,1)}, u32[]{:S(2)}) copy-start(bf16[2560]{0:T(1024)(128)(2,1)} %param.21) | copy-start | bytes 15364
  7.2 8.1 %copy-start.6 = (bf16[512]{0:T(512)(128)(2,1)S(1)}, bf16[512]{0:T(512)(128)(2,1)}, u32[]{:S(2)}) copy-start(bf16[512]{0:T(512)(128)(2,1)} %param.22) | copy-start | bytes 3076
  7.2 8.1 %copy-start.7 = (bf16[512]{0:T(512)(128)(2,1)S(1)}, bf16[512]{0:T(512)(128)(2,1)}, u32[]{:S(2)}) copy-start(bf16[512]{0:T(512)(128)(2,1)} %param.23) | copy-start | bytes 3076
  7.3 70.2 %all-gather.6.cloned.1.call-start = ((), (), s32[]{:S(2)}) async-start(), calls=%async_computation | async-start | bytes 2785280 | tf_op jit(solution)/shard_map/all_gather | solution.py:74
  8.0 142.2 %all-gather.10.cloned.1.call-start = ((), (), s32[]{:S(2)}) async-start(), calls=%async_computation.2 | async-start | bytes 2785280 | tf_op jit(solution)/shard_map/all_gather | solution.py:75
  8.7 298.8 %all-gather.8.cloned.1.call-start = ((), (), s32[]{:S(2)}) async-start(), calls=%async_computation.1 | async-start | bytes 13926400 | tf_op jit(solution)/shard_map/all_gather | solution.py:73
  9.5 353.3 %all-gather.12.cloned.1.call-start = ((), (), s32[]{:S(2)}) async-start(), calls=%async_computation.3 | async-start | bytes 2228224 | tf_op jit(solution)/shard_map/all_gather | solution.py:109
  11.2 407.5 %all-gather.14.cloned.1.call-start = ((), (), s32[]{:S(2)}) async-start(), calls=%async_computation.4 | async-start | bytes 2228224 | tf_op jit(solution)/shard_map/all_gather | solution.py:110
  152.8 154.7 %copy-start.3 = (f32[256,512]{1,0:T(8,128)}, f32[256,512]{1,0:T(8,128)S(1)}, u32[]{:S(2)}) copy-start(f32[256,512]{1,0:T(8,128)S(1)} %convolution_add_fusion.1) | copy-start | bytes 1572868
  320.0 1.4 copy-start.1
  321.4 1.5 copy-start
  324.0 94.6 %copy-start.4 = (s32[20,2,4]{0,2,1:T(4,128)S(1)}, s32[20,2,4]{0,2,1:T(4,128)}, u32[]{:S(2)}) copy-start(s32[20,2,4]{0,2,1:T(4,128)} %param.26) | copy-start | bytes 1924
Sparse Core Ops, SparseCore 0:
  9.9 67.5 all-gather.5
  79.3 70.8 all-gather.9
  152.0 155.5 all-gather.7
  309.9 52.7 all-gather.11
  365.1 53.4 all-gather.13
where the time goes:
time: 525 us; the launch traced here: 524 us
  waiting for transfers between devices  377 us (72%)
  matrix products  75.4 us (14%)
  local copies, waits for them, and re-layouts  37.5 us (7%)
  other arithmetic  17.8 us (3%)
  between operations  14.8 us (3%)
    all_gather x1, waiting for transfers between devices, on_device(): lax.all_gather(w_query, 'grp', axis=0, tiled=True)  154 us
    all_gather x1, waiting for transfers between devices, on_device(): lax.all_gather(w_value, 'grp', axis=0, tiled=True)  68.9 us
    all_gather x1, waiting for transfers between devices, on_device(): lax.all_gather(w_key, 'grp', axis=0, tiled=True)  62.1 us
    all_gather x1, waiting for transfers between devices, on_device(): piece_values = lax.all_gather(cache_values, 'ctx', axis=0, tiled=True)  55.9 us
    all_gather x1, waiting for transfers between devices, on_device(): piece_keys = lax.all_gather(cache_keys, 'ctx', axis=0, tiled=True)  34 us
    dot_general x16, matrix products, one_key_block(): jnp.einsum('rkgd,pkd->kgrp', query_heads, block_keys) * score_scale  30.5 us
    dot_general x16, matrix products, one_key_block(): jnp.einsum('kgrp,pkd->kgrd', weights, block_values)  28.4 us
    dynamic_slice x16, local copies, waits for them, and re-layouts, one_key_block(): lax.dynamic_slice_in_dim(piece_values, block_step * QBLK, QBLK, 0)  15.9 us
  transfers between devices with their start and end apart: 5, of which 5 were waited for; matrix products, arithmetic and copies ran while one was open for 6% of the time, Pallas kernels for 0%

commit v1 on v0

v1 whole, which is shorter than its diff:
```python
import functools
import math

import jax
import jax.numpy as jnp
import numpy as np
from jax import lax
from jax.experimental import pallas as pl
from jax.experimental.pallas import tpu as pltpu
from jax.sharding import PartitionSpec as P

MESH = pl.DeviceIdType.MESH

HD = 128
GROUP = 5
QBLK = 128
SEL = 4

norm_eps = 1e-06
rope_base = 10000000.0

NX, NY, NZ = 4, 4, 8
CHUNKS = 11
AHEAD = 3
SLOTS = CHUNKS + 4


def angle_tables(head_dim):
    half_dim = head_dim // 2
    frequency = rope_base ** (-2.0 * np.arange(half_dim) / head_dim)
    tables = np.stack(
        [np.mod(frequency * 32.0**digit_level, 2.0 * np.pi) for digit_level in range(4)]
    )
    return np.concatenate([tables, tables], axis=1)


def device_of(x, y, z, core):
    return (x * 4 + (y // 2) * 2 + core, (y % 2) * NZ + z)


def kernel(
    start_ref,
    tok_ref,
    wq_ref,
    wk_ref,
    wv_ref,
    ck_ref,
    cv_ref,
    lists_ref,
    gain_ref,
    bias_ref,
    table_ref,
    ctx_ref,
    keys_ref,
    values_ref,
    wbuf,
    kvbuf,
    tokbuf,
    normed,
    cosine,
    sine,
    qbuf,
    knew,
    vnew,
    ostage,
    lvmem,
    lsmem,
    load_sem,
    z_recv,
    y_recv,
    z_send,
    y_send,
    x_recv,
    x_send,
    kv_load,
    kv_recv,
    kv_send,
    misc_sem,
    misc_send,
    out_local,
    out_send,
    out_recv,
):
    ctx = lax.axis_index("ctx")
    grp = lax.axis_index("grp")
    core = ctx % 2
    y_hi = (ctx // 2) % 2
    x = ctx // 4
    y_lo = grp // NZ
    z = grp % NZ
    y = y_hi * 2 + y_lo
    rows = tok_ref.shape[0]

    partner = device_of(x, y, z, 1 - core)
    xp = device_of((x + 1) % NX, y, z, core)
    xm = device_of((x + 3) % NX, y, z, core)
    yp = device_of(x, (y + 1) % NY, z, core)
    ym = device_of(x, (y + 3) % NY, z, core)
    zp = device_of(x, y, (z + 1) % NZ, core)
    zm = device_of(x, y, (z + 7) % NZ, core)
    ykv = device_of(x, (y + 3 + 2 * (y % 2)) % NY, z, core)

    def remote(src, dst, send_sem, recv_sem, device):
        return pltpu.make_async_remote_copy(
            src_ref=src,
            dst_ref=dst,
            send_sem=send_sem,
            recv_sem=recv_sem,
            device_id=device,
            device_id_type=MESH,
        )

    def columns(index):
        return pl.ds(pl.multiple_of(index * HD, HD), HD)

    def slot_of(i):
        return jnp.where(i == 0, 10 + x, i - 1)

    tok_load = pltpu.make_async_copy(tok_ref, tokbuf.at[0], misc_sem.at[0])
    loads = []
    for i in range(CHUNKS):
        if i == 0:
            src, dst = wq_ref.at[:, columns(core * 10 + x)], wbuf.at[10 + x, grp]
        elif i <= 4:
            ref = wk_ref if i % 2 == 1 else wv_ref
            src, dst = ref.at[:, columns(core * 2 + (i - 1) // 2)], wbuf.at[i - 1, grp]
        else:
            src, dst = wq_ref.at[:, columns(core * 10 + i - 1)], wbuf.at[i - 1, grp]
        loads.append(pltpu.make_async_copy(src, dst, load_sem.at[i]))
    kv_loads = []
    for part in range(4):
        ref = ck_ref if part < 2 else cv_ref
        kv_loads.append(
            pltpu.make_async_copy(
                ref.at[:, columns(core * 2 + part % 2)], kvbuf.at[ctx, part], kv_load.at[part]
            )
        )
    list_load = pltpu.make_async_copy(lists_ref, lsmem.at[0], misc_sem.at[3])
    for copy in kv_loads + loads[:AHEAD] + [tok_load, list_load] + loads[AHEAD:]:
        copy.start()

    barrier = pltpu.get_barrier_semaphore()
    for device in (partner, xp, xm, yp, ym, zp, zm):
        pl.semaphore_signal(barrier, inc=1, device_id=device, device_id_type=MESH)
    pl.semaphore_wait(barrier, 7)

    half = wbuf.shape[2] // 2

    def send_y(i, slot, shard):
        row = y_lo * NZ + shard
        lower, upper = wbuf.at[slot, row, 0:half], wbuf.at[slot, row, half : 2 * half]
        remote(lower, lower, y_send.at[i], y_recv.at[i], yp).start()
        remote(upper, upper, y_send.at[i], y_recv.at[i], ym).start()

    def z_copies(i, slot, step):
        from_left = wbuf.at[slot, y_lo * NZ + (z + 8 - step) % NZ]
        from_right = wbuf.at[slot, y_lo * NZ + (z + step) % NZ]
        if step == 4:
            from_left, from_right = from_left.at[0:half], from_right.at[half : 2 * half]
        return (
            remote(from_left, from_left, z_send.at[i], z_recv.at[i, step - 1], zp),
            remote(from_right, from_right, z_send.at[i], z_recv.at[i, 3 + step], zm),
        )

    def send_z(i, slot, step):
        to_right = wbuf.at[slot, y_lo * NZ + (z + 9 - step) % NZ]
        to_left = wbuf.at[slot, y_lo * NZ + (z + step - 1) % NZ]
        if step == 4:
            to_right, to_left = to_right.at[0:half], to_left.at[half : 2 * half]
        remote(to_right, to_right, z_send.at[i], z_recv.at[i, step - 1], zp).start()
        remote(to_left, to_left, z_send.at[i], z_recv.at[i, 3 + step], zm).start()

    def send_own(i, slot):
        send_z(i, slot, 1)
        send_y(i, slot, z)

    def pass_on(i, step):
        slot = slot_of(i)
        left, right = z_copies(i, slot, step)
        left.wait_recv()
        right.wait_recv()
        if step < 4:
            send_z(i, slot, step + 1)
            send_y(i, slot, (z + 8 - step) % NZ)
            send_y(i, slot, (z + step) % NZ)
        else:
            send_y(i, slot, (z + 4) % NZ)

    def wait_y(i):
        landed = wbuf.at[slot_of(i), pl.ds((1 - y_lo) * NZ, NZ)]
        remote(landed, landed, y_send.at[i], y_recv.at[i], yp).wait_recv()

    kv_parts = []
    for part in range(4):
        ref = ck_ref if part < 2 else cv_ref
        kv_parts.append(
            remote(
                ref.at[:, columns((1 - core) * 2 + part % 2)],
                kvbuf.at[ctx, part],
                kv_send.at[0],
                kv_recv.at[0],
                partner,
            )
        )

    def pair(at_x, at_y):
        return kvbuf.at[pl.ds(at_x * 4 + at_y * 2, 2)]

    left_x, right_x, far_x = (x + 3) % NX, (x + 1) % NX, (x + 2) % NX
    kv_y = remote(pair(x, y_hi), pair(x, y_hi), kv_send.at[1], kv_recv.at[1], ykv)
    kv_x = [
        remote(pair(x, y_hi), pair(x, y_hi), kv_send.at[2], kv_recv.at[2], xp),
        remote(pair(x, y_hi), pair(x, y_hi), kv_send.at[3], kv_recv.at[3], xm),
        remote(pair(x, 1 - y_hi), pair(x, 1 - y_hi), kv_send.at[4], kv_recv.at[4], xp),
        remote(pair(x, 1 - y_hi), pair(x, 1 - y_hi), kv_send.at[5], kv_recv.at[5], xm),
        remote(pair(left_x, y_hi), pair(left_x, y_hi), kv_send.at[6], kv_recv.at[6], xp),
        remote(
            pair(right_x, 1 - y_hi), pair(right_x, 1 - y_hi), kv_send.at[7], kv_recv.at[7], xm
        ),
    ]

    def shared(at_x, upper):
        return wbuf.at[10 + at_x, 8:16] if upper else wbuf.at[10 + at_x, 0:8]

    x_copies = [
        remote(shared(x, 0), shared(x, 0), x_send.at[0], x_recv.at[0], xp),
        remote(shared(x, 1), shared(x, 1), x_send.at[1], x_recv.at[1], xm),
        remote(shared(x, 1), shared(x, 1), x_send.at[2], x_recv.at[2], xp),
        remote(shared(x, 0), shared(x, 0), x_send.at[3], x_recv.at[3], xm),
        remote(shared(left_x, 0), shared(left_x, 0), x_send.at[4], x_recv.at[4], xp),
        remote(shared(right_x, 1), shared(right_x, 1), x_send.at[5], x_recv.at[5], xm),
    ]

    def norm_rows(part):
        @pl.loop(0, rows // 16)
        def _(step):
            at = pl.ds(pl.multiple_of(step * 16, 16), 16)
            wide = tokbuf[part, at, :].astype(jnp.float32)
            mean = jnp.mean(wide * wide, axis=-1, keepdims=True)
            scaled = wide * lax.rsqrt(mean + norm_eps) * gain_ref[0:1, :]
            normed[pl.ds(pl.multiple_of(part * rows + step * 16, 16), 16), :] = scaled.astype(
                jnp.bfloat16
            )

    def tables():
        lane = lax.broadcasted_iota(jnp.int32, (QBLK, HD), 1)
        sign = jnp.where(lane < HD // 2, -1.0, 1.0)

        @pl.loop(0, 2 * rows // QBLK)
        def _(step):
            of_ctx = jnp.where(step < rows // QBLK, ctx, ctx + 1 - 2 * core)
            first = (of_ctx * 16 + grp) * rows + (step % (rows // QBLK)) * QBLK
            position = start_ref[0] + first + lax.broadcasted_iota(jnp.int32, (QBLK, HD), 0)
            angle = jnp.zeros((QBLK, HD), jnp.float32)
            for level in range(4):
                digit = ((position >> (5 * level)) & 31).astype(jnp.float32)
                angle = angle + digit * table_ref[level : level + 1, :]
            turns = jnp.floor(angle * (1.0 / (2.0 * math.pi)) + 0.5)
            angle = (angle - turns * 6.28125) - turns * (2.0 * math.pi - 6.28125)
            at = pl.ds(pl.multiple_of(step * QBLK, QBLK), QBLK)
            cosine[at, :] = jnp.cos(angle)
            sine[at, :] = jnp.sin(angle) * sign

    def project(slot, bias_row):
        weights = wbuf[slot].reshape(normed.shape[1], HD)
        linear = jnp.dot(normed[...], weights, preferred_element_type=jnp.float32)
        return linear + bias_ref[pl.ds(bias_row, 1), :]

    def rope(linear):
        return linear * cosine[...] + pltpu.roll(linear, HD // 2, 1) * sine[...]

    def copy_out(slot, out_ref, column):
        own, other = ostage.at[slot, 0:rows], ostage.at[slot, rows : 2 * rows]
        target = out_ref.at[:, columns(column)]
        remote(other, target, out_send.at[0], out_recv.at[0], partner).start()
        pltpu.make_async_copy(own, target, out_local.at[0]).start()

    def key_chunk(head):
        result = rope(project(2 * head, 20 + core * 2 + head))
        knew[head] = result.astype(jnp.bfloat16)
        ostage[2 * head] = result
        copy_out(2 * head, keys_ref, core * 2 + head)

    def value_chunk(head):
        result = project(2 * head + 1, 24 + core * 2 + head)
        vnew[head] = result.astype(jnp.bfloat16)
        ostage[2 * head + 1] = result
        copy_out(2 * head + 1, values_ref, core * 2 + head)

    scale = HD**-0.5 * math.log2(math.e)
    row_at = lax.broadcasted_iota(jnp.int32, (QBLK, QBLK), 0)
    column_at = lax.broadcasted_iota(jnp.int32, (QBLK, QBLK), 1)

    def query_chunk(slot):
        local = slot % 10
        head = local // GROUP
        qbuf[...] = (rope(project(slot, core * 10 + local)) * scale).astype(jnp.bfloat16)
        for block in range(2 * rows // QBLK):
            side, part = block // (rows // QBLK), block % (rows // QBLK)
            at = slice(block * QBLK, (block + 1) * QBLK)
            entry = ((core * 10 + local) * (rows // QBLK) + part) * SEL
            keys, values, shifts = [], [], []
            for step in range(SEL):
                index = lsmem[side, (entry + step) // HD, (entry + step) % HD]
                shifts.append(jnp.where(index >= 0, 0.0, -jnp.inf))
                index = jnp.maximum(index, 0)
                keys.append(kvbuf[index, head])
                values.append(kvbuf[index, 2 + head])
            keys.append(knew[head, at, :])
            values.append(vnew[head, at, :])
            scores = lax.dot_general(
                qbuf[at, :],
                jnp.concatenate(keys, axis=0),
                (((1,), (1,)), ((), ())),
                preferred_element_type=jnp.float32,
            )
            parts = [
                scores[:, step * QBLK : (step + 1) * QBLK] + shifts[step] for step in range(SEL)
            ]
            near = scores[:, SEL * QBLK :]
            parts.append(jnp.where(row_at >= column_at, near, -jnp.inf))
            scores = jnp.concatenate(parts, axis=1)
            weights = jnp.exp2(scores - jnp.max(scores, axis=1, keepdims=True))
            total = jnp.sum(weights, axis=1, keepdims=True)
            mixed = jnp.dot(
                weights.astype(jnp.bfloat16),
                jnp.concatenate(values, axis=0),
                preferred_element_type=jnp.float32,
            )
            ostage[slot, at, :] = mixed * (1.0 / total)
        copy_out(slot, ctx_ref, core * 10 + local)

    tok_send = remote(tok_ref, tokbuf.at[1], misc_send.at[0], misc_sem.at[1], partner)
    list_send = remote(lists_ref, lvmem, misc_send.at[1], misc_sem.at[2], partner)
    for copy in kv_parts:
        copy.start()
    for i in range(AHEAD):
        loads[i].wait()
        send_own(i, 10 + x if i == 0 else i - 1)
    for copy in kv_loads:
        copy.wait()
    both = kvbuf.at[ctx + 1 - 2 * core]
    remote(both, both, kv_send.at[0], kv_recv.at[0], partner).wait_recv()
    kv_y.start()
    kv_x[0].start()
    kv_x[1].start()
    list_send.start()
    tok_send.start()
    for i in range(AHEAD, CHUNKS):
        loads[i].wait()
    tok_load.wait()
    norm_rows(0)

    @pl.loop(0, SLOTS)
    def _(now):
        @pl.when(now + AHEAD < CHUNKS)
        def _():
            send_own(now + AHEAD, now + AHEAD - 1)

        for step in (4, 3, 2, 1):

            @pl.when((now >= step - 1) & (now < CHUNKS + step - 1))
            def _():
                pass_on(now - (step - 1), step)

        @pl.when(now == 1)
        def _():
            other = pair(x, 1 - y_hi)
            remote(other, other, kv_send.at[1], kv_recv.at[1], ykv).wait_recv()
            kv_x[2].start()
            kv_x[3].start()
            here = pair(left_x, y_hi)
            remote(here, here, kv_send.at[2], kv_recv.at[2], xp).wait_recv()
            kv_x[4].start()

        @pl.when(now == 3)
        def _():
            here = pair(right_x, 1 - y_hi)
            remote(here, here, kv_send.at[5], kv_recv.at[5], xm).wait_recv()
            kv_x[5].start()

        @pl.when(now == 0)
        def _():
            tables()

        @pl.when(now == 1)
        def _():
            tok_send.wait_recv()
            norm_rows(1)

        @pl.when(now == 2)
        def _():
            list_send.wait_recv()
            list_load.wait()
            move = pltpu.make_async_copy(lvmem, lsmem.at[1], misc_sem.at[4])
            move.start()
            move.wait()

        @pl.when(now >= 4)
        def _():
            wait_y(now - 4)

        @pl.when(now == 4)
        def _():
            for copy in x_copies[:4]:
                copy.start()

        for head in range(2):

            @pl.when(now == 5 + 2 * head)
            def _():
                key_chunk(head)

            @pl.when(now == 6 + 2 * head)
            def _():
                value_chunk(head)

        @pl.when(now == 8)
        def _():
            here, there = shared(left_x, 0), shared(right_x, 1)
            remote(here, here, x_send.at[0], x_recv.at[0], xp).wait_recv()
            x_copies[4].start()
            remote(there, there, x_send.at[1], x_recv.at[1], xm).wait_recv()
            x_copies[5].start()
            for landed, sem in (
                (pair(right_x, y_hi), 3),
                (pair(left_x, 1 - y_hi), 4),
                (pair(far_x, y_hi), 6),
                (pair(far_x, 1 - y_hi), 7),
            ):
                remote(landed, landed, kv_send.at[sem], kv_recv.at[sem], xp).wait_recv()

        @pl.when(now == 12)
        def _():
            here = shared(left_x, 1)
            remote(here, here, x_send.at[2], x_recv.at[2], xp).wait_recv()

        @pl.when(now == 13)
        def _():
            here = shared(right_x, 0)
            remote(here, here, x_send.at[3], x_recv.at[3], xm).wait_recv()

        @pl.when(now == 14)
        def _():
            here, there = shared(far_x, 0), shared(far_x, 1)
            remote(here, here, x_send.at[4], x_recv.at[4], xp).wait_recv()
            remote(there, there, x_send.at[5], x_recv.at[5], xm).wait_recv()

        extra = jnp.where(now == 9, 0, jnp.where(now == 12, 3, jnp.where(now == 13, 1, 2)))
        jobs = jnp.where(now >= 9, jnp.where((now == 10) | (now == 11), 1, 2), 0)

        def job(which, carry):
            query_chunk(jnp.where(which == 0, now - 5, 10 + (x + extra) % NX))
            return carry

        lax.fori_loop(0, jobs, job, 0)

    @pl.loop(0, CHUNKS)
    def _(i):
        sent = wbuf.at[0, 0:7]
        pltpu.make_async_copy(sent, sent, z_send.at[i]).wait()
        sent = wbuf.at[0, 0:8]
        pltpu.make_async_copy(sent, sent, y_send.at[i]).wait()

    for copy in x_copies:
        copy.wait_send()
    pltpu.make_async_copy(kvbuf.at[0], kvbuf.at[0], kv_send.at[0]).wait()
    kv_y.wait_send()
    for copy in kv_x:
        copy.wait_send()
    tok_send.wait_send()
    list_send.wait_send()
    written = ostage.at[0:7]
    pltpu.make_async_copy(written, written, out_local.at[0]).wait()
    pltpu.make_async_copy(written, written, out_send.at[0]).wait()
    pltpu.make_async_copy(written, written, out_recv.at[0]).wait()


def on_device(
    tokens,
    norm_gain,
    w_query,
    w_key,
    w_value,
    b_query,
    b_key,
    b_value,
    cache_keys,
    cache_values,
    block_lists,
    start_position,
):
    rows, features = tokens.shape
    shard = w_query.shape[0]
    bias = jnp.concatenate([b_query, b_key, b_value]).astype(jnp.float32).reshape(28, HD)
    bias = jnp.pad(bias, ((0, 4), (0, 0)))
    gain = jnp.broadcast_to(norm_gain.astype(jnp.float32)[None, :], (8, features))
    lists = jnp.pad(block_lists.reshape(-1), (0, 1024 - block_lists.size)).reshape(8, HD)
    table = jnp.asarray(np.pad(angle_tables(HD), ((0, 4), (0, 0))), jnp.float32)
    hbm = pl.BlockSpec(memory_space=pl.ANY)
    vmem = pl.BlockSpec(memory_space=pltpu.VMEM)
    smem = pl.BlockSpec(memory_space=pltpu.SMEM)
    dma = pltpu.SemaphoreType.DMA
    return pl.pallas_call(
        kernel,
        out_shape=(
            jax.ShapeDtypeStruct((rows, 20 * HD), jnp.float32),
            jax.ShapeDtypeStruct((rows, 4 * HD), jnp.float32),
            jax.ShapeDtypeStruct((rows, 4 * HD), jnp.float32),
        ),
        in_specs=[smem] + [hbm] * 6 + [vmem] * 4,
        out_specs=[hbm] * 3,
        scratch_shapes=[
            pltpu.VMEM((14, 16, shard, HD), jnp.bfloat16),
            pltpu.VMEM((16, 4, QBLK, HD), jnp.bfloat16),
            pltpu.VMEM((2, rows, features), jnp.bfloat16),
            pltpu.VMEM((2 * rows, features), jnp.bfloat16),
            pltpu.VMEM((2 * rows, HD), jnp.float32),
            pltpu.VMEM((2 * rows, HD), jnp.float32),
            pltpu.VMEM((2 * rows, HD), jnp.bfloat16),
            pltpu.VMEM((2, 2 * rows, HD), jnp.bfloat16),
            pltpu.VMEM((2, 2 * rows, HD), jnp.bfloat16),
            pltpu.VMEM((14, 2 * rows, HD), jnp.float32),
            pltpu.VMEM((8, HD), jnp.int32),
            pltpu.SMEM((2, 8, HD), jnp.int32),
            dma((CHUNKS,)),
            dma((CHUNKS, 8)),
            dma((CHUNKS,)),
            dma((CHUNKS,)),
            dma((CHUNKS,)),
            dma((6,)),
            dma((6,)),
            dma((4,)),
            dma((8,)),
            dma((8,)),
            dma((5,)),
            dma((2,)),
            dma((1,)),
            dma((1,)),
            dma((1,)),
        ],
        compiler_params=pltpu.CompilerParams(
            collective_id=0, has_side_effects=True, vmem_limit_bytes=48 << 20
        ),
        name="gather_attend",
    )(
        start_position,
        tokens,
        w_query,
        w_key,
        w_value,
        cache_keys,
        cache_values,
        lists,
        gain,
        bias,
        table,
    )


def solution(mesh):
    in_specs = (
        P(("ctx", "grp"), None),
        P(),
        P("grp", None),
        P("grp", None),
        P("grp", None),
        P(),
        P(),
        P(),
        P("ctx", None),
        P("ctx", None),
        P(None, ("ctx", "grp"), None),
        P(),
    )
    out_specs = (P(("ctx", "grp"), None), P(("ctx", "grp"), None), P(("ctx", "grp"), None))
    return jax.shard_map(
        on_device, mesh=mesh, in_specs=in_specs, out_specs=out_specs, check_vma=False
    )
```

time: 525 us -> 104 us (0.20)
  waiting for transfers between devices: 377 us -> 0 us
  Pallas kernels: 0 us -> 88.2 us
  matrix products: 75.4 us -> 0 us
  local copies, waits for them, and re-layouts: 37.5 us -> 13.4 us
  other arithmetic: 17.8 us -> 0.74 us
  between operations: 14.8 us -> 1.31 us
    all_gather x5 -> x0, waiting for transfers between devices: 375 us -> none  [the longest x1 154 us: on_device(): lax.all_gather(w_query, 'grp', axis=0, tiled=True)]
    pallas_call x0 -> x1, Pallas kernels: none -> 88.2 us  [on_device(): pl.pallas_call(kernel, out_shape=(jax.ShapeDtypeStruct((rows, 20 * HD), j...]
    dot_general x37 -> x0, matrix products: 75.4 us -> none  [the longest x16 30.5 us: one_key_block(): jnp.einsum('rkgd,pkd->kgrp', query_heads, block_keys) * score_scale]
    dynamic_slice x16 -> x0, local copies, waits for them, and re-layouts: 15.9 us -> none  [one_key_block(): lax.dynamic_slice_in_dim(piece_values, block_step * QBLK, QBLK, 0)]
    reduce_sum x18 -> x0, other arithmetic: 12.4 us -> none  [the longest x16 9.74 us: one_key_block(): new_total = old_total * factor + jnp.sum(weights, axis=-1)]
    unnamed x28 -> x18, local copies, waits for them, and re-layouts: 7.84 us -> 12.6 us
  transfers between devices with their start and end apart: 5 -> 0, of which waited for: 5 -> 0; matrix products, arithmetic and copies ran while one was open for 6% -> 0% of each run, Pallas kernels for 0% -> 0%
where the time goes in v1:
time: 104 us
  Pallas kernels  88.2 us (85%)
  local copies, waits for them, and re-layouts  13.4 us (13%)
  between operations  1.31 us (1%)
    pallas_call x1, Pallas kernels, on_device(): pl.pallas_call(kernel, out_shape=(jax.ShapeDtypeStruct((rows, 20 * HD), j...  88.2 us
    unnamed x18, local copies, waits for them, and re-layouts  12.6 us

profile of v1, /device:TPU:1, one launch (start us, length us, event | category | flops | bytes accessed | tf_op | source)
XLA Modules:
  0.0 103.6 jit_solution(3806049733349723467)
XLA Ops:
  1.3 0.7 maximum_bitcast_fusion
  2.0 0.8 copy.16
  2.8 0.1 reshape.17
  2.9 0.7 broadcast_in_dim.2.gain_ref
  3.6 0.0 copy-start
  3.6 1.3 %copy-done = bf16[256,2560]{1,0:T(8,128)(2,1)S(1)} copy-done((bf16[256,2560]{1,0:T(8,128)(2,1)S(1)}, bf16[256,2560]{1,0:T(8,128)(2,1)}, u32[]{:S(2)}) %copy-start) | copy-done | bytes 1310744
  4.9 0.0 copy-start.1
  4.9 1.1 %copy-done.1 = bf16[160,2560]{1,0:T(8,128)(2,1)S(1)} copy-done((bf16[160,2560]{1,0:T(8,128)(2,1)S(1)}, bf16[160,2560]{1,0:T(8,128)(2,1)}, u32[]{:S(2)}) %copy-start.1) | copy-done | bytes 819224
  6.1 0.0 copy-start.2
  6.1 0.9 copy-done.2
  7.0 0.0 copy-start.3
  7.0 0.9 copy-done.3
  7.9 0.0 copy-start.4
  7.9 0.9 copy-done.4
  8.8 0.0 copy-start.5
  8.8 0.9 copy-done.5
  9.7 0.0 copy-start.6
  9.7 0.7 copy-done.6
  10.4 88.2 %gather_attend.1 = (f32[256,2560]{1,0:T(8,128)}, f32[256,512]{1,0:T(8,128)S(1)}, f32[256,512]{1,0:T(8,128)S(1)}) custom-call(s32[1]{0:T(128)S(6)} %copy.20.start_ref, bf16[256,2560]{1,0:T(8,128)(2,1)S(1)} %copy-done, bf16[160,2560]{1,0:T(8,128)(2,1)S(1)} %copy-done.1, bf16[160,512]{1,0:T(8,128)(2,1)S(1)} %copy-done.2, bf16[160,512]{1,0:T(8,128)(2,1)S(1)} %copy-done.3, ...), custom_call_target="tpu_custom_call" | custom-call | tf_op jit(solution)/shard_map/gather_attend/pallas_call | solution.py:504
  98.6 3.4 %copy.21 = f32[256,2560]{1,0:T(8,128)} copy(f32[256,2560]{1,0:T(8,128)} %get-tuple-element.6) | data formatting | bytes 5242880
  102.0 0.8 copy.22
  102.8 0.8 copy.23
  (2 shorter events, 0.0 us)
Async XLA Ops:
  3.6 1.3 %copy-start = (bf16[256,2560]{1,0:T(8,128)(2,1)S(1)}, bf16[256,2560]{1,0:T(8,128)(2,1)}, u32[]{:S(2)}) copy-start(bf16[256,2560]{1,0:T(8,128)(2,1)} %tok_ref.1) | copy-start | bytes 3932164
  4.9 1.1 %copy-start.1 = (bf16[160,2560]{1,0:T(8,128)(2,1)S(1)}, bf16[160,2560]{1,0:T(8,128)(2,1)}, u32[]{:S(2)}) copy-start(bf16[160,2560]{1,0:T(8,128)(2,1)} %wq_ref.1) | copy-start | bytes 2457604
  6.1 0.9 copy-start.2
  7.0 0.9 copy-start.3
  7.9 0.9 copy-start.4
  8.8 0.9 copy-start.5
  9.7 0.7 copy-start.6

commit v2 on v1

v2 whole, which is shorter than its diff:
```python
import functools
import math

import jax
import jax.numpy as jnp
import numpy as np
from jax import lax
from jax.experimental import pallas as pl
from jax.experimental.pallas import tpu as pltpu
from jax.sharding import PartitionSpec as P

MESH = pl.DeviceIdType.MESH

HD = 128
GROUP = 5
QBLK = 128
SEL = 4

norm_eps = 1e-06
rope_base = 10000000.0

NX, NY, NZ = 4, 4, 8
CHUNKS = 11
PLACE = (None, 0, 1, 4, 2, 3, 5, 6, 7, 8, 9)

Y_FIRST = (8,)
SCHEDULE = (
    ((
        ("own", 0), ("own", 1),
    ), ("N0",)),
    ((
        ("own", 2), ("own", 3),
    ), ("T",)),
    ((
        ("kv0",), ("own", 4),
    ), ("N1",)),
    ((
        ("z", 0, 1, 0), ("z", 1, 1, 0), ("z", 2, 1, 0), ("z", 3, 1, 0), ("z", 4, 1, 0),
        ("z", 0, 2, 0), ("z", 1, 2, 0), ("z", 2, 2, 0), ("z", 3, 2, 0), ("kv1",), ("kv2",),
        ("z", 4, 2, 0), ("z", 0, 3, 0), ("z", 1, 3, 0), ("own", 5), ("z", 2, 3, 0),
        ("z", 3, 3, 0), ("own", 6), ("z", 4, 3, 0), ("z", 0, 4, 0), ("z", 1, 4, 0), ("own", 7),
        ("z", 5, 1, 0), ("z", 2, 4, 0), ("z", 3, 4, 0), ("own", 8), ("kv3",), ("z", 6, 1, 0),
        ("z", 4, 4, 0), ("own", 9), ("z", 7, 1, 0), ("z", 5, 2, 0), ("z", 8, 1, 0),
        ("z", 6, 2, 0), ("b0",), ("z", 9, 1, 0), ("z", 7, 2, 0), ("z", 5, 3, 0), ("y", 1),
        ("y", 2),
    ), ("K", 0)),
    ((
        ("own", 10), ("z", 6, 3, 0), ("yf", 8), ("z", 8, 2, 0), ("y", 3), ("kvw",),
    ), ("P", 0)),
    ((
        ("z", 7, 3, 0), ("z", 5, 4, 0), ("z", 9, 2, 0),
    ), ("A", 0)),
    ((
        ("z", 10, 1, 0),
    ), ("A", 1)),
    ((
        ("z", 6, 4, 0), ("z", 8, 1, 1), ("z", 8, 3, 0), ("z", 7, 4, 0), ("b1",), ("z", 9, 3, 0),
        ("z", 10, 2, 0), ("y", 4), ("y", 5),
    ), ("K", 1)),
    ((
        ("z", 8, 2, 1), ("z", 8, 4, 0), ("z", 9, 4, 0), ("y", 6), ("y", 7),
    ), ("P", 1)),
    ((
        ("z", 10, 3, 0),
    ), ("A", 2)),
    ((

    ), ("A", 3)),
    ((
        ("z", 8, 3, 1), ("b2",),
    ), ("P", 3)),
    ((
        ("z", 10, 4, 0),
    ), ("A", 6)),
    ((

    ), ("A", 7)),
    ((
        ("z", 8, 4, 1), ("y", 8), ("y", 9),
    ), ("P", 2)),
    ((

    ), ("A", 4)),
    ((

    ), ("A", 5)),
    ((
        ("y", 10), ("b3",),
    ), ("P", 4)),
    ((

    ), ("A", 8)),
    ((

    ), ("A", 9)),
)
AHEAD = sum(op[0] == "own" for op in SCHEDULE[0][0])


def angle_tables(head_dim):
    half_dim = head_dim // 2
    frequency = rope_base ** (-2.0 * np.arange(half_dim) / head_dim)
    tables = np.stack(
        [np.mod(frequency * 32.0**digit_level, 2.0 * np.pi) for digit_level in range(4)]
    )
    return np.concatenate([tables, tables], axis=1)


def device_of(x, y, z, core):
    return (x * 4 + (y // 2) * 2 + core, (y % 2) * NZ + z)


def kernel(
    start_ref,
    tok_ref,
    wq_ref,
    wk_ref,
    wv_ref,
    ck_ref,
    cv_ref,
    lists_ref,
    prep_ref,
    table_hbm,
    ctx_ref,
    keys_ref,
    values_ref,
    wbuf,
    kvbuf,
    tokbuf,
    normed,
    cosine,
    sine,
    qbuf,
    knew,
    vnew,
    ostage,
    gain_ref,
    table_ref,
    lvmem,
    lsmem,
    load_sem,
    z_recv,
    z_recv_across,
    y_recv,
    z_send,
    y_send,
    x_recv,
    x_send,
    kv_load,
    kv_recv,
    kv_send,
    misc_sem,
    misc_send,
    out_local,
    out_send,
    out_recv,
):
    ctx = lax.axis_index("ctx")
    grp = lax.axis_index("grp")
    core = ctx % 2
    y_hi = (ctx // 2) % 2
    x = ctx // 4
    y_lo = grp // NZ
    z = grp % NZ
    y = y_hi * 2 + y_lo
    rows = tok_ref.shape[0]

    partner = device_of(x, y, z, 1 - core)
    xp = device_of((x + 1) % NX, y, z, core)
    xm = device_of((x + 3) % NX, y, z, core)
    yp = device_of(x, (y + 1) % NY, z, core)
    ym = device_of(x, (y + 3) % NY, z, core)
    zp = device_of(x, y, (z + 1) % NZ, core)
    zm = device_of(x, y, (z + 7) % NZ, core)
    ykv = device_of(x, (y + 3 + 2 * (y % 2)) % NY, z, core)
    yother = device_of(x, (y + 1 + 2 * (y % 2)) % NY, z, core)

    def remote(src, dst, send_sem, recv_sem, device):
        return pltpu.make_async_remote_copy(
            src_ref=src,
            dst_ref=dst,
            send_sem=send_sem,
            recv_sem=recv_sem,
            device_id=device,
            device_id_type=MESH,
        )

    def columns(index):
        return pl.ds(pl.multiple_of(index * HD, HD), HD)

    def slot_of(i):
        return 10 + x if i == 0 else PLACE[i]

    tok_load = pltpu.make_async_copy(tok_ref, tokbuf.at[0], misc_sem.at[0])
    loads = []
    for i in range(CHUNKS):
        place = PLACE[i]
        if i == 0:
            src = wq_ref.at[:, columns(core * 10 + x)]
        elif place < 4:
            ref = wk_ref if place % 2 == 0 else wv_ref
            src = ref.at[:, columns(core * 2 + place // 2)]
        else:
            src = wq_ref.at[:, columns(core * 10 + place)]
        loads.append(pltpu.make_async_copy(src, wbuf.at[slot_of(i), grp], load_sem.at[i]))
    kv_loads = []
    for part in range(4):
        ref = ck_ref if part < 2 else cv_ref
        kv_loads.append(
            pltpu.make_async_copy(
                ref.at[:, columns(core * 2 + part % 2)], kvbuf.at[ctx, part], kv_load.at[part]
            )
        )
    list_load = pltpu.make_async_copy(lists_ref, lsmem.at[0], misc_sem.at[3])
    table_load = pltpu.make_async_copy(table_hbm, table_ref, misc_sem.at[5])
    for copy in kv_loads + loads[:AHEAD] + [tok_load, list_load, table_load] + loads[AHEAD:]:
        copy.start()

    barrier = pltpu.get_barrier_semaphore()
    for device in (partner, xp, xm, yp, ym, zp, zm):
        pl.semaphore_signal(barrier, inc=1, device_id=device, device_id_type=MESH)
    pl.semaphore_wait(barrier, 7)

    shard_rows = wbuf.shape[2]
    half = shard_rows // 2

    def send_y(i, slot, shard, distance):
        row = y_lo * NZ + shard
        cut = half - 16 if distance <= 1 else half
        lower, upper = wbuf.at[slot, row, 0:cut], wbuf.at[slot, row, cut:shard_rows]
        remote(lower, lower, y_send.at[i], y_recv.at[i], ykv).start()
        remote(upper, upper, y_send.at[i], y_recv.at[i], yother).start()

    def send_z(i, slot, distance, line, wait=False):
        base = (y_lo if line == 0 else 1 - y_lo) * NZ
        back = 0 if wait else 1
        rightward = wbuf.at[slot, base + (z + 8 - distance + back) % NZ]
        leftward = wbuf.at[slot, base + (z + distance - back) % NZ]
        if distance == 4:
            rightward, leftward = rightward.at[0:half], leftward.at[half:shard_rows]
        recv = [
            z_recv.at[i, n] if line == 0 else z_recv_across.at[n]
            for n in (distance - 1, 3 + distance)
        ]
        copies = (
            remote(rightward, rightward, z_send.at[i], recv[0], zp),
            remote(leftward, leftward, z_send.at[i], recv[1], zm),
        )
        for copy in copies:
            if wait:
                copy.wait_recv()
            else:
                copy.start()

    def send_own(i):
        slot = slot_of(i)
        loads[i].wait()
        send_z(i, slot, 1, 0)
        send_y(i, slot, z, 0)

    def pass_on(i, distance, line):
        slot = slot_of(i)
        send_z(i, slot, distance, line, wait=True)
        if distance < 4:
            send_z(i, slot, distance + 1, line)
        if i in Y_FIRST:
            return
        send_y(i, slot, (z + 8 - distance) % NZ, distance)
        if distance < 4:
            send_y(i, slot, (z + distance) % NZ, distance)

    def send_across(i):
        slot = slot_of(i)
        landed = wbuf.at[slot, (1 - y_lo) * NZ + z]
        remote(landed, landed, y_send.at[i], y_recv.at[i], ykv).wait_recv()
        send_z(i, slot, 1, 1)

    def wait_y(i):
        if i in Y_FIRST:
            return
        landed = wbuf.at[slot_of(i), pl.ds((1 - y_lo) * NZ, NZ)]
        remote(landed, landed, y_send.at[i], y_recv.at[i], ykv).wait_recv()

    kv_parts = []
    for part in range(4):
        ref = ck_ref if part < 2 else cv_ref
        kv_parts.append(
            remote(
                ref.at[:, columns((1 - core) * 2 + part % 2)],
                kvbuf.at[ctx, part],
                kv_send.at[0],
                kv_recv.at[0],
                partner,
            )
        )

    def pair(at_x, at_y):
        return kvbuf.at[pl.ds(at_x * 4 + at_y * 2, 2)]

    left_x, right_x, far_x = (x + 3) % NX, (x + 1) % NX, (x + 2) % NX
    kv_y = remote(pair(x, y_hi), pair(x, y_hi), kv_send.at[1], kv_recv.at[1], ykv)
    kv_x = [
        remote(pair(x, y_hi), pair(x, y_hi), kv_send.at[2], kv_recv.at[2], xp),
        remote(pair(x, y_hi), pair(x, y_hi), kv_send.at[3], kv_recv.at[3], xm),
        remote(pair(x, 1 - y_hi), pair(x, 1 - y_hi), kv_send.at[4], kv_recv.at[4], xp),
        remote(pair(x, 1 - y_hi), pair(x, 1 - y_hi), kv_send.at[5], kv_recv.at[5], xm),
        remote(pair(left_x, y_hi), pair(left_x, y_hi), kv_send.at[6], kv_recv.at[6], xp),
        remote(
            pair(right_x, 1 - y_hi), pair(right_x, 1 - y_hi), kv_send.at[7], kv_recv.at[7], xm
        ),
    ]

    def shared(at_x, upper):
        return wbuf.at[10 + at_x, 8:16] if upper else wbuf.at[10 + at_x, 0:8]

    x_copies = [
        remote(shared(x, 0), shared(x, 0), x_send.at[0], x_recv.at[0], xp),
        remote(shared(x, 1), shared(x, 1), x_send.at[1], x_recv.at[1], xm),
        remote(shared(x, 1), shared(x, 1), x_send.at[2], x_recv.at[2], xp),
        remote(shared(x, 0), shared(x, 0), x_send.at[3], x_recv.at[3], xm),
        remote(shared(left_x, 0), shared(left_x, 0), x_send.at[4], x_recv.at[4], xp),
        remote(shared(right_x, 1), shared(right_x, 1), x_send.at[5], x_recv.at[5], xm),
    ]

    def norm_rows(part):
        @pl.loop(0, rows // 64)
        def _(step):
            at = pl.ds(pl.multiple_of(step * 64, 64), 64)
            wide = tokbuf[part, at, :].astype(jnp.float32)
            mean = jnp.mean(wide * wide, axis=-1, keepdims=True)
            scaled = wide * lax.rsqrt(mean + norm_eps) * gain_ref[0:1, :]
            normed[pl.ds(pl.multiple_of(part * rows + step * 64, 64), 64), :] = scaled.astype(
                jnp.bfloat16
            )

    def tables():
        lane = lax.broadcasted_iota(jnp.int32, (QBLK, HD), 1)
        sign = jnp.where(lane < HD // 2, -1.0, 1.0)

        @pl.loop(0, 2 * rows // QBLK)
        def _(step):
            of_ctx = jnp.where(step < rows // QBLK, ctx, ctx + 1 - 2 * core)
            first = (of_ctx * 16 + grp) * rows + (step % (rows // QBLK)) * QBLK
            position = start_ref[0] + first + lax.broadcasted_iota(jnp.int32, (QBLK, HD), 0)
            angle = jnp.zeros((QBLK, HD), jnp.float32)
            for level in range(4):
                digit = ((position >> (5 * level)) & 31).astype(jnp.float32)
                angle = angle + digit * table_ref[level : level + 1, :]
            turns = jnp.floor(angle * (1.0 / (2.0 * math.pi)) + 0.5)
            angle = (angle - turns * 6.28125) - turns * (2.0 * math.pi - 6.28125)
            at = pl.ds(pl.multiple_of(step * QBLK, QBLK), QBLK)
            cosine[at, :] = jnp.cos(angle)
            sine[at, :] = jnp.sin(angle) * sign

    def project(slots, bias_rows):
        weights = [wbuf[slot].reshape(normed.shape[1], HD) for slot in slots]
        linear = jnp.dot(
            normed[...], jnp.concatenate(weights, axis=1), preferred_element_type=jnp.float32
        )
        return [
            linear[:, n * HD : (n + 1) * HD] + prep_ref[pl.ds(20 + row, 1), :]
            for n, row in enumerate(bias_rows)
        ]

    def rope(linear):
        return linear * cosine[...] + pltpu.roll(linear, HD // 2, 1) * sine[...]

    def copy_out(slot, out_ref, column):
        own, other = ostage.at[slot, 0:rows], ostage.at[slot, rows : 2 * rows]
        target = out_ref.at[:, columns(column)]
        remote(other, target, out_send.at[0], out_recv.at[0], partner).start()
        pltpu.make_async_copy(own, target, out_local.at[0]).start()

    def key_value_chunks(head):
        global_head = core * 2 + head
        linear_key, linear_value = project(
            (2 * head, 2 * head + 1), (20 + global_head, 24 + global_head)
        )
        key = rope(linear_key)
        knew[head] = key.astype(jnp.bfloat16)
        ostage[2 * head] = key
        copy_out(2 * head, keys_ref, global_head)
        vnew[head] = linear_value.astype(jnp.bfloat16)
        ostage[2 * head + 1] = linear_value
        copy_out(2 * head + 1, values_ref, global_head)

    scale = HD**-0.5 * math.log2(math.e)
    row_at = lax.broadcasted_iota(jnp.int32, (QBLK, QBLK), 0)
    column_at = lax.broadcasted_iota(jnp.int32, (QBLK, QBLK), 1)
    blocks = rows // QBLK

    def attend(n, slot):
        local = slot % 10
        head = local // GROUP
        scores, values = [], []
        for block in range(2 * blocks):
            at = slice(block * QBLK, (block + 1) * QBLK)
            keys, shifts = [], []
            values.append([])
            for step in range(SEL):
                index = lsmem[block // blocks, block % blocks, step, core * 10 + local]
                shifts.append(jnp.where(index >= 0, 0.0, -jnp.inf))
                index = jnp.maximum(index, 0)
                keys.append(kvbuf[index, head])
                values[-1].append(kvbuf[index, 2 + head])
            keys.append(knew[head, at, :])
            values[-1].append(vnew[head, at, :])
            all_keys = lax.dot_general(
                qbuf[n, at, :],
                jnp.concatenate(keys, axis=0),
                (((1,), (1,)), ((), ())),
                preferred_element_type=jnp.float32,
            )
            parts = [
                all_keys[:, step * QBLK : (step + 1) * QBLK] + shifts[step] for step in range(SEL)
            ]
            near = all_keys[:, SEL * QBLK :]
            scores.append(parts + [jnp.where(row_at >= column_at, near, -jnp.inf)])
        largest = [
            jnp.max(functools.reduce(jnp.maximum, parts), axis=1, keepdims=True)
            for parts in scores
        ]
        for block in range(2 * blocks):
            at = slice(block * QBLK, (block + 1) * QBLK)
            weights = [jnp.exp2(part - largest[block]) for part in scores[block]]
            total = jnp.sum(functools.reduce(jnp.add, weights), axis=1, keepdims=True)
            mixed = jnp.dot(
                jnp.concatenate([part.astype(jnp.bfloat16) for part in weights], axis=1),
                jnp.concatenate(values[block], axis=0),
                preferred_element_type=jnp.float32,
            )
            ostage[slot, at, :] = mixed * (1.0 / total)
        copy_out(slot, ctx_ref, core * 10 + local)

    def query_chunks(first, second):
        heads = (core * 10 + first % 10, core * 10 + second % 10)
        linear = project((first, second), heads)
        for n in range(2):
            qbuf[n] = (rope(linear[n]) * scale).astype(jnp.bfloat16)

    tok_send = remote(tok_ref, tokbuf.at[1], misc_send.at[0], misc_sem.at[1], partner)
    list_send = remote(lists_ref, lvmem, misc_send.at[1], misc_sem.at[2], partner)

    def kv_wait(landed, number):
        remote(landed, landed, kv_send.at[number], kv_recv.at[number], xp).wait_recv()

    def shared_wait(landed, number):
        remote(landed, landed, x_send.at[number], x_recv.at[number], xp).wait_recv()

    def run(op):
        kind, at = op[0], op[1:]
        if kind == "own":
            send_own(*at)
        elif kind == "z":
            pass_on(*at)
        elif kind == "yf":
            send_across(*at)
        elif kind == "y":
            wait_y(*at)
        elif kind == "kv0":
            for copy in kv_loads:
                copy.wait()
            kv_wait(kvbuf.at[ctx + 1 - 2 * core], 0)
            kv_y.start()
            kv_x[0].start()
            kv_x[1].start()
        elif kind == "kv1":
            kv_wait(pair(x, 1 - y_hi), 1)
            kv_x[2].start()
            kv_x[3].start()
        elif kind == "kv2":
            kv_wait(pair(left_x, y_hi), 2)
            kv_x[4].start()
        elif kind == "kv3":
            kv_wait(pair(right_x, 1 - y_hi), 5)
            kv_x[5].start()
        elif kind == "kvw":
            kv_wait(pair(right_x, y_hi), 3)
            kv_wait(pair(left_x, 1 - y_hi), 4)
            kv_wait(pair(far_x, y_hi), 6)
            kv_wait(pair(far_x, 1 - y_hi), 7)
        elif kind == "b0":
            wait_y(0)
            for copy in x_copies[:4]:
                copy.start()
        elif kind == "b1":
            shared_wait(shared(left_x, 0), 0)
            shared_wait(shared(right_x, 1), 1)
            x_copies[4].start()
            x_copies[5].start()
        elif kind == "b2":
            shared_wait(shared(left_x, 1), 2)
            shared_wait(shared(right_x, 0), 3)
        elif kind == "b3":
            shared_wait(shared(far_x, 0), 4)
            shared_wait(shared(far_x, 1), 5)

    for copy in kv_parts:
        copy.start()
    for op in SCHEDULE[0][0][:AHEAD]:
        run(op)
    list_send.start()
    tok_send.start()
    table_load.wait()
    for step in range(gain_ref.shape[1] // HD):
        gain_ref[0:1, step * HD : (step + 1) * HD] = prep_ref[step : step + 1, :]

    pairs = (
        (10 + x, 4),
        (5, 6),
        (7, 8),
        (10 + left_x, 10 + right_x),
        (9, 10 + far_x),
    )
    units = [unit for _, unit in SCHEDULE]

    @pl.loop(0, len(SCHEDULE))
    def _(now):
        for number, (ops, _unused) in enumerate(SCHEDULE):
            rest = ops[AHEAD:] if number == 0 else ops
            if rest:

                @pl.when(now == number)
                def _():
                    for op in rest:
                        run(op)

        def on(kind):
            places = [n for n, unit in enumerate(units) if unit[0] == kind]
            condition = functools.reduce(jnp.logical_or, [now == n for n in places])

            def pick(values):
                value = values[units[places[-1]][1]]
                for n in places[:-1]:
                    value = jnp.where(now == n, values[units[n][1]], value)
                return value

            return condition, pick

        @pl.when(on("N0")[0])
        def _():
            tok_load.wait()
            norm_rows(0)

        @pl.when(on("T")[0])
        def _():
            tables()

        @pl.when(on("N1")[0])
        def _():
            tok_send.wait_recv()
            norm_rows(1)
            list_send.wait_recv()
            list_load.wait()
            move = pltpu.make_async_copy(lvmem, lsmem.at[1], misc_sem.at[4])
            move.start()
            move.wait()

        condition, pick_pair = on("K")

        @pl.when(condition)
        def _():
            key_value_chunks(pick_pair((0, 1)))

        condition, pick_query = on("P")

        @pl.when(condition)
        def _():
            query_chunks(
                pick_query([first for first, _ in pairs]),
                pick_query([second for _, second in pairs]),
            )

        condition, pick_head = on("A")

        @pl.when(condition)
        def _():
            flat = [slot for both in pairs for slot in both]
            attend(pick_head([n % 2 for n in range(len(flat))]), pick_head(flat))

    for i in range(CHUNKS):
        sent = wbuf.at[0, 0:14] if i in Y_FIRST else wbuf.at[0, 0:7]
        pltpu.make_async_copy(sent, sent, z_send.at[i]).wait()
        sent = wbuf.at[0, 0] if i in Y_FIRST else wbuf.at[0, 0:8]
        pltpu.make_async_copy(sent, sent, y_send.at[i]).wait()

    for copy in x_copies:
        copy.wait_send()
    pltpu.make_async_copy(kvbuf.at[0], kvbuf.at[0], kv_send.at[0]).wait()
    kv_y.wait_send()
    for copy in kv_x:
        copy.wait_send()
    tok_send.wait_send()
    list_send.wait_send()
    written = ostage.at[0:7]
    pltpu.make_async_copy(written, written, out_local.at[0]).wait()
    pltpu.make_async_copy(written, written, out_send.at[0]).wait()
    pltpu.make_async_copy(written, written, out_recv.at[0]).wait()


def on_device(
    tokens,
    norm_gain,
    w_query,
    w_key,
    w_value,
    b_query,
    b_key,
    b_value,
    cache_keys,
    cache_values,
    block_lists,
    start_position,
):
    rows, features = tokens.shape
    shard = w_query.shape[0]
    prep = jnp.concatenate([norm_gain, b_query, b_key, b_value]).reshape(48, HD)
    prep = prep.astype(jnp.float32)
    lists = jnp.transpose(block_lists, (1, 2, 0))
    table = jnp.asarray(np.pad(angle_tables(HD), ((0, 4), (0, 0))), jnp.float32)
    hbm = pl.BlockSpec(memory_space=pltpu.HBM)
    vmem = pl.BlockSpec(memory_space=pltpu.VMEM)
    smem = pl.BlockSpec(memory_space=pltpu.SMEM)
    dma = pltpu.SemaphoreType.DMA
    return pl.pallas_call(
        kernel,
        out_shape=(
            jax.ShapeDtypeStruct((rows, 20 * HD), jnp.float32),
            jax.ShapeDtypeStruct((rows, 4 * HD), jnp.float32),
            jax.ShapeDtypeStruct((rows, 4 * HD), jnp.float32),
        ),
        in_specs=[smem] + [hbm] * 7 + [vmem] + [hbm],
        out_specs=[hbm] * 3,
        scratch_shapes=[
            pltpu.VMEM((14, 16, shard, HD), jnp.bfloat16),
            pltpu.VMEM((16, 4, QBLK, HD), jnp.bfloat16),
            pltpu.VMEM((2, rows, features), jnp.bfloat16),
            pltpu.VMEM((2 * rows, features), jnp.bfloat16),
            pltpu.VMEM((2 * rows, HD), jnp.float32),
            pltpu.VMEM((2 * rows, HD), jnp.float32),
            pltpu.VMEM((2, 2 * rows, HD), jnp.bfloat16),
            pltpu.VMEM((2, 2 * rows, HD), jnp.bfloat16),
            pltpu.VMEM((2, 2 * rows, HD), jnp.bfloat16),
            pltpu.VMEM((14, 2 * rows, HD), jnp.float32),
            pltpu.VMEM((8, features), jnp.float32),
            pltpu.VMEM((8, HD), jnp.float32),
            pltpu.VMEM(lists.shape, jnp.int32),
            pltpu.SMEM((2,) + lists.shape, jnp.int32),
            dma((CHUNKS,)),
            dma((CHUNKS, 8)),
            dma((8,)),
            dma((CHUNKS,)),
            dma((CHUNKS,)),
            dma((CHUNKS,)),
            dma((6,)),
            dma((6,)),
            dma((4,)),
            dma((8,)),
            dma((8,)),
            dma((6,)),
            dma((2,)),
            dma((1,)),
            dma((1,)),
            dma((1,)),
        ],
        compiler_params=pltpu.CompilerParams(
            collective_id=0, has_side_effects=True, vmem_limit_bytes=58 << 20
        ),
        name="gather_attend",
    )(
        start_position,
        tokens,
        w_query,
        w_key,
        w_value,
        cache_keys,
        cache_values,
        lists,
        prep,
        table,
    )


def solution(mesh):
    in_specs = (
        P(("ctx", "grp"), None),
        P(),
        P("grp", None),
        P("grp", None),
        P("grp", None),
        P(),
        P(),
        P(),
        P("ctx", None),
        P("ctx", None),
        P(None, ("ctx", "grp"), None),
        P(),
    )
    out_specs = (P(("ctx", "grp"), None), P(("ctx", "grp"), None), P(("ctx", "grp"), None))
    return jax.shard_map(
        on_device, mesh=mesh, in_specs=in_specs, out_specs=out_specs, check_vma=False
    )
```

time: 104 us -> 74 us (0.71)
  Pallas kernels: 88.2 us -> 66 us
  local copies, waits for them, and re-layouts: 13.4 us -> 5.09 us
    pallas_call x1, Pallas kernels: 88.2 us -> 66 us  [on_device(): pl.pallas_call(kernel, out_shape=(jax.ShapeDtypeStruct((rows, 20 * HD), j...]
    unnamed x18 -> x7, local copies, waits for them, and re-layouts: 12.6 us -> 5.09 us
where the time goes in v2:
time: 74 us; the launch traced here: 73.8 us
  Pallas kernels  66 us (89%)
  local copies, waits for them, and re-layouts  5.09 us (7%)
  other arithmetic  1.36 us (2%)
  between operations  1.31 us (2%)
    pallas_call x1, Pallas kernels, on_device(): pl.pallas_call(kernel, out_shape=(jax.ShapeDtypeStruct((rows, 20 * HD), j...  66 us
    unnamed x7, local copies, waits for them, and re-layouts  5.09 us

profile of v2, /device:TPU:1, one launch (start us, length us, event | category | flops | bytes accessed | tf_op | source)
XLA Modules:
  0.0 73.8 jit_solution(11424020766544506918)
XLA Ops:
  1.3 1.4 %fusion.prep_ref = f32[48,128]{1,0:T(8,128)} fusion(bf16[512]{0:T(512)(128)(2,1)} %param.20, bf16[512]{0:T(512)(128)(2,1)} %param.19, bf16[2560]{0:T(1024)(128)(2,1)} %param.18, bf16[2560]{0:T(1024)(128)(2,1)} %param.14), kind=kLoop, calls=%fused_computation.1 | loop fusion | flops 55296 | bytes 36864 | tf_op jit(solution)/shard_map/convert_element_type | solution.py:618
  2.6 66.0 %gather_attend.1 = (f32[256,2560]{1,0:T(8,128)}, f32[256,512]{1,0:T(8,128)}, f32[256,512]{1,0:T(8,128)}) custom-call(s32[1]{0:T(128)S(6)} %copy.19.start_ref, bf16[256,2560]{1,0:T(8,128)(2,1)} %tok_ref.1, bf16[160,2560]{1,0:T(8,128)(2,1)} %wq_ref.1, bf16[160,512]{1,0:T(8,128)(2,1)} %wk_ref.1, bf16[160,512]{1,0:T(8,128)(2,1)} %wv_ref.1, ...), custom_call_target="tpu_custom_call" | custom-call | tf_op jit(solution)/shard_map/gather_attend/pallas_call | solution.py:625
  68.7 0.0 copy-start.1
  68.7 0.0 copy-start
  68.7 3.5 %copy.20 = f32[256,2560]{1,0:T(8,128)} copy(f32[256,2560]{1,0:T(8,128)} %get-tuple-element.6) | data formatting | bytes 5242880
  72.2 0.0 copy-done.1
  72.2 0.8 %copy.21 = f32[256,512]{1,0:T(8,128)} copy(f32[256,512]{1,0:T(8,128)S(1)} %copy-done.1) | data formatting | bytes 1048576
  73.0 0.0 copy-done
  73.0 0.8 %copy.22 = f32[256,512]{1,0:T(8,128)} copy(f32[256,512]{1,0:T(8,128)S(1)} %copy-done) | data formatting | bytes 1048576
Async XLA Ops:
  68.7 3.5 %copy-start.1 = (f32[256,512]{1,0:T(8,128)S(1)}, f32[256,512]{1,0:T(8,128)}, u32[]{:S(2)}) copy-start(f32[256,512]{1,0:T(8,128)} %get-tuple-element.7) | copy-start | bytes 1572868
  68.7 4.3 %copy-start = (f32[256,512]{1,0:T(8,128)S(1)}, f32[256,512]{1,0:T(8,128)}, u32[]{:S(2)}) copy-start(f32[256,512]{1,0:T(8,128)} %get-tuple-element.8) | copy-start | bytes 1572868

commit v3 on v2

--- a/solution.py
+++ b/solution.py
@@ -119,11 +119,12 @@
     ck_ref,
     cv_ref,
     lists_ref,
-    prep_ref,
+    gain_hbm,
+    bq_hbm,
+    bk_hbm,
+    bv_hbm,
     table_hbm,
-    ctx_ref,
-    keys_ref,
-    values_ref,
+    out_ref,
     wbuf,
     kvbuf,
     tokbuf,
@@ -135,6 +136,11 @@
     vnew,
     ostage,
     gain_ref,
+    bias_ref,
+    flat_gain,
+    flat_bq,
+    flat_bk,
+    flat_bv,
     table_ref,
     lvmem,
     lsmem,
@@ -151,7 +157,6 @@
     kv_send,
     misc_sem,
     misc_send,
-    out_local,
     out_send,
     out_recv,
 ):
@@ -213,7 +218,18 @@
         )
     list_load = pltpu.make_async_copy(lists_ref, lsmem.at[0], misc_sem.at[3])
     table_load = pltpu.make_async_copy(table_hbm, table_ref, misc_sem.at[5])
-    for copy in kv_loads + loads[:AHEAD] + [tok_load, list_load, table_load] + loads[AHEAD:]:
+    flat_loads = [
+        pltpu.make_async_copy(src, dst, misc_sem.at[6 + n])
+        for n, (src, dst) in enumerate(
+            (
+                (gain_hbm, flat_gain),
+                (bq_hbm, flat_bq),
+                (bk_hbm, flat_bk),
+                (bv_hbm, flat_bv),
+            )
+        )
+    ]
+    for copy in kv_loads + loads[:AHEAD] + [tok_load] + flat_loads + [table_load, list_load] + loads[AHEAD:]:
         copy.start()
 
     barrier = pltpu.get_barrier_semaphore()
@@ -358,18 +374,16 @@
             normed[...], jnp.concatenate(weights, axis=1), preferred_element_type=jnp.float32
         )
         return [
-            linear[:, n * HD : (n + 1) * HD] + prep_ref[pl.ds(20 + row, 1), :]
+            linear[:, n * HD : (n + 1) * HD] + bias_ref[pl.ds(row, 1), :]
             for n, row in enumerate(bias_rows)
         ]
 
     def rope(linear):
         return linear * cosine[...] + pltpu.roll(linear, HD // 2, 1) * sine[...]
 
-    def copy_out(slot, out_ref, column):
-        own, other = ostage.at[slot, 0:rows], ostage.at[slot, rows : 2 * rows]
-        target = out_ref.at[:, columns(column)]
+    def copy_out(slot, place):
+        other, target = ostage.at[slot], out_ref.at[place]
         remote(other, target, out_send.at[0], out_recv.at[0], partner).start()
-        pltpu.make_async_copy(own, target, out_local.at[0]).start()
 
     def key_value_chunks(head):
         global_head = core * 2 + head
@@ -378,11 +392,13 @@
         )
         key = rope(linear_key)
         knew[head] = key.astype(jnp.bfloat16)
-        ostage[2 * head] = key
-        copy_out(2 * head, keys_ref, global_head)
+        ostage[2 * head] = key[rows:]
+        copy_out(2 * head, 20 + global_head)
+        out_ref[20 + global_head] = key[:rows]
         vnew[head] = linear_value.astype(jnp.bfloat16)
-        ostage[2 * head + 1] = linear_value
-        copy_out(2 * head + 1, values_ref, global_head)
+        ostage[2 * head + 1] = linear_value[rows:]
+        copy_out(2 * head + 1, 24 + global_head)
+        out_ref[24 + global_head] = linear_value[:rows]
 
     scale = HD**-0.5 * math.log2(math.e)
     row_at = lax.broadcasted_iota(jnp.int32, (QBLK, QBLK), 0)
@@ -420,8 +436,7 @@
             jnp.max(functools.reduce(jnp.maximum, parts), axis=1, keepdims=True)
             for parts in scores
         ]
-        for block in range(2 * blocks):
-            at = slice(block * QBLK, (block + 1) * QBLK)
+        for block in list(range(blocks, 2 * blocks)) + list(range(blocks)):
             weights = [jnp.exp2(part - largest[block]) for part in scores[block]]
             total = jnp.sum(functools.reduce(jnp.add, weights), axis=1, keepdims=True)
             mixed = jnp.dot(
@@ -429,8 +444,14 @@
                 jnp.concatenate(values[block], axis=0),
                 preferred_element_type=jnp.float32,
             )
-            ostage[slot, at, :] = mixed * (1.0 / total)
-        copy_out(slot, ctx_ref, core * 10 + local)
+            result = mixed * (1.0 / total)
+            at = slice(block % blocks * QBLK, (block % blocks + 1) * QBLK)
+            if block >= blocks:
+                ostage[slot, at, :] = result
+            else:
+                out_ref[core * 10 + local, at, :] = result
+            if block == 2 * blocks - 1:
+                copy_out(slot, core * 10 + local)
 
     def query_chunks(first, second):
         heads = (core * 10 + first % 10, core * 10 + second % 10)
@@ -502,8 +523,15 @@
     list_send.start()
     tok_send.start()
     table_load.wait()
-    for step in range(gain_ref.shape[1] // HD):
-        gain_ref[0:1, step * HD : (step + 1) * HD] = prep_ref[step : step + 1, :]
+    for copy in flat_loads:
+        copy.wait()
+    gain_ref[0:1, :] = flat_gain[...].astype(jnp.float32).reshape(1, gain_ref.shape[1])
+    row = 0
+    for flat in (flat_bq, flat_bk, flat_bv):
+        for step in range(flat.shape[0] // HD):
+            piece = flat[step * HD : (step + 1) * HD].astype(jnp.float32)
+            bias_ref[row : row + 1, :] = piece.reshape(1, HD)
+            row += 1
 
     pairs = (
         (10 + x, 4),
@@ -592,10 +620,27 @@
         copy.wait_send()
     tok_send.wait_send()
     list_send.wait_send()
-    written = ostage.at[0:7]
-    pltpu.make_async_copy(written, written, out_local.at[0]).wait()
+    written = ostage
     pltpu.make_async_copy(written, written, out_send.at[0]).wait()
     pltpu.make_async_copy(written, written, out_recv.at[0]).wait()
+
+
+def write_kernel(source, ctx_ref, keys_ref, values_ref, sem):
+    copies = []
+    for place in range(28):
+        target, first = ((ctx_ref, 0), (keys_ref, 20), (values_ref, 24))[
+            (place >= 20) + (place >= 24)
+        ]
+        column = (place - first) * HD
+        copies.append(
+            pltpu.make_async_copy(
+                source.at[place], target.at[:, column : column + HD], sem.at[place]
+            )
+        )
+    for copy in copies:
+        copy.start()
+    for copy in copies:
+        copy.wait()
 
 
 def on_device(
@@ -614,23 +659,17 @@
 ):
     rows, features = tokens.shape
     shard = w_query.shape[0]
-    prep = jnp.concatenate([norm_gain, b_query, b_key, b_value]).reshape(48, HD)
-    prep = prep.astype(jnp.float32)
     lists = jnp.transpose(block_lists, (1, 2, 0))
     table = jnp.asarray(np.pad(angle_tables(HD), ((0, 4), (0, 0))), jnp.float32)
     hbm = pl.BlockSpec(memory_space=pltpu.HBM)
     vmem = pl.BlockSpec(memory_space=pltpu.VMEM)
     smem = pl.BlockSpec(memory_space=pltpu.SMEM)
     dma = pltpu.SemaphoreType.DMA
-    return pl.pallas_call(
+    heads_out = pl.pallas_call(
         kernel,
-        out_shape=(
-            jax.ShapeDtypeStruct((rows, 20 * HD), jnp.float32),
-            jax.ShapeDtypeStruct((rows, 4 * HD), jnp.float32),
-            jax.ShapeDtypeStruct((rows, 4 * HD), jnp.float32),
-        ),
-        in_specs=[smem] + [hbm] * 7 + [vmem] + [hbm],
-        out_specs=[hbm] * 3,
+        out_shape=pltpu.VMEM((28, rows, HD), jnp.float32),
+        in_specs=[smem] + [hbm] * 12,
+        out_specs=pl.BlockSpec(memory_space=pltpu.VMEM),
         scratch_shapes=[
             pltpu.VMEM((14, 16, shard, HD), jnp.bfloat16),
             pltpu.VMEM((16, 4, QBLK, HD), jnp.bfloat16),
@@ -641,8 +680,13 @@
             pltpu.VMEM((2, 2 * rows, HD), jnp.bfloat16),
             pltpu.VMEM((2, 2 * rows, HD), jnp.bfloat16),
             pltpu.VMEM((2, 2 * rows, HD), jnp.bfloat16),
-            pltpu.VMEM((14, 2 * rows, HD), jnp.float32),
+            pltpu.VMEM((14, rows, HD), jnp.float32),
             pltpu.VMEM((8, features), jnp.float32),
+            pltpu.VMEM((32, HD), jnp.float32),
+            pltpu.VMEM(norm_gain.shape, jnp.bfloat16),
+            pltpu.VMEM(b_query.shape, jnp.bfloat16),
+            pltpu.VMEM(b_key.shape, jnp.bfloat16),
+            pltpu.VMEM(b_value.shape, jnp.bfloat16),
             pltpu.VMEM((8, HD), jnp.float32),
             pltpu.VMEM(lists.shape, jnp.int32),
             pltpu.SMEM((2,) + lists.shape, jnp.int32),
@@ -657,9 +701,8 @@
             dma((4,)),
             dma((8,)),
             dma((8,)),
-            dma((6,)),
+            dma((10,)),
             dma((2,)),
-            dma((1,)),
             dma((1,)),
             dma((1,)),
         ],
@@ -676,9 +719,25 @@
         cache_keys,
         cache_values,
         lists,
-        prep,
+        norm_gain,
+        b_query,
+        b_key,
+        b_value,
         table,
     )
+    return pl.pallas_call(
+        write_kernel,
+        out_shape=(
+            jax.ShapeDtypeStruct((rows, 20 * HD), jnp.float32),
+            jax.ShapeDtypeStruct((rows, 4 * HD), jnp.float32),
+            jax.ShapeDtypeStruct((rows, 4 * HD), jnp.float32),
+        ),
+        in_specs=[vmem],
+        out_specs=[hbm] * 3,
+        scratch_shapes=[dma((28,))],
+        compiler_params=pltpu.CompilerParams(vmem_limit_bytes=4 << 20),
+        name="write_out",
+    )(heads_out)
 
 
 def solution(mesh):

time: 74 us -> 69.2 us (0.935)
  local copies, waits for them, and re-layouts: 5.09 us -> 0 us
  Pallas kernels: 66 us -> 67.8 us
  other arithmetic: 1.36 us -> 0 us
    unnamed x7 -> x0, local copies, waits for them, and re-layouts: 5.09 us -> none
    pallas_call x1 -> x2, Pallas kernels: 66 us -> 67.8 us  [the longest x1 65.8 us: on_device(): pl.pallas_call(kernel, out_shape=pltpu.VMEM((28, rows, HD), jnp.float32),...]
    convert_element_type x1 -> x0, other arithmetic: 1.36 us -> none  [on_device(): prep = prep.astype(jnp.float32)]
where the time goes in v3:
time: 69.2 us; the launch traced here: 69.1 us
  Pallas kernels  67.8 us (98%)
  between operations  1.29 us (2%)
    pallas_call x1, Pallas kernels, on_device(): pl.pallas_call(kernel, out_shape=pltpu.VMEM((28, rows, HD), jnp.float32),...  65.8 us
    pallas_call x1, Pallas kernels, on_device(): pl.pallas_call(write_kernel, out_shape=(jax.ShapeDtypeStruct((rows, 20 *...  2.06 us

profile of v3, /device:TPU:1, one launch (start us, length us, event | category | flops | bytes accessed | tf_op | source)
XLA Modules:
  0.0 69.1 jit_solution(7342021545385902717)
XLA Ops:
  1.3 65.8 %gather_attend.1.source = f32[28,256,128]{2,1,0:T(8,128)S(1)} custom-call(s32[1]{0:T(128)S(6)} %copy.16.start_ref, bf16[256,2560]{1,0:T(8,128)(2,1)} %tok_ref.1, bf16[160,2560]{1,0:T(8,128)(2,1)} %wq_ref.1, bf16[160,512]{1,0:T(8,128)(2,1)} %wk_ref.1, bf16[160,512]{1,0:T(8,128)(2,1)} %wv_ref.1, bf16[128,512]{1,0:T(8,128)(2,1)} %ck_ref.1, ...), custom_call_target="tpu_custom_call" | custom-call | tf_op jit(solution)/shard_map/gather_attend/pallas_call | solution.py:668
  67.1 2.1 %write_out.1 = (f32[256,2560]{1,0:T(8,128)}, f32[256,512]{1,0:T(8,128)}, f32[256,512]{1,0:T(8,128)}) custom-call(f32[28,256,128]{2,1,0:T(8,128)S(1)} %gather_attend.1.source), custom_call_target="tpu_custom_call" | custom-call | tf_op jit(solution)/shard_map/write_out/pallas_call | solution.py:728

commit v4 on v3

--- a/solution.py
+++ b/solution.py
@@ -24,77 +24,62 @@
 PLACE = (None, 0, 1, 4, 2, 3, 5, 6, 7, 8, 9)
 
 Y_FIRST = (8,)
+NEAR = 1
 SCHEDULE = (
     ((
-        ("own", 0), ("own", 1),
+        ("own", 0), ("own", 3), ("kv0", 0), ("own", 1), ("own", 5), ("own", 2), ("kv0", 1),
+        ("z", 0, 1, 0), ("z", 3, 1, 0),
     ), ("N0",)),
     ((
-        ("own", 2), ("own", 3),
+        ("own", 4), ("z", 5, 1, 0), ("z", 1, 1, 0), ("kv1", 0),
     ), ("T",)),
     ((
-        ("kv0",), ("own", 4),
+        ("z", 0, 2, 0), ("z", 2, 1, 0), ("z", 3, 2, 0), ("kv2", 0), ("z", 4, 1, 0), ("kv1", 1),
+        ("z", 1, 2, 0), ("z", 0, 3, 0), ("own", 7), ("own", 6), ("z", 2, 2, 0), ("own", 8),
+        ("kv3", 0), ("kv2", 1), ("z", 0, 4, 0), ("z", 4, 2, 0), ("z", 3, 3, 0), ("kv3", 1),
+        ("z", 5, 2, 0), ("z", 1, 3, 0), ("z", 2, 3, 0), ("z", 7, 1, 0), ("b0",), ("own", 9),
     ), ("N1",)),
     ((
-        ("z", 0, 1, 0), ("z", 1, 1, 0), ("z", 2, 1, 0), ("z", 3, 1, 0), ("z", 4, 1, 0),
-        ("z", 0, 2, 0), ("z", 1, 2, 0), ("z", 2, 2, 0), ("z", 3, 2, 0), ("kv1",), ("kv2",),
-        ("z", 4, 2, 0), ("z", 0, 3, 0), ("z", 1, 3, 0), ("own", 5), ("z", 2, 3, 0),
-        ("z", 3, 3, 0), ("own", 6), ("z", 4, 3, 0), ("z", 0, 4, 0), ("z", 1, 4, 0), ("own", 7),
-        ("z", 5, 1, 0), ("z", 2, 4, 0), ("z", 3, 4, 0), ("own", 8), ("kv3",), ("z", 6, 1, 0),
-        ("z", 4, 4, 0), ("own", 9), ("z", 7, 1, 0), ("z", 5, 2, 0), ("z", 8, 1, 0),
-        ("z", 6, 2, 0), ("b0",), ("z", 9, 1, 0), ("z", 7, 2, 0), ("z", 5, 3, 0), ("y", 1),
-        ("y", 2),
+        ("yf", 8), ("own", 10), ("z", 3, 4, 0), ("z", 2, 4, 0), ("z", 4, 3, 0), ("z", 1, 4, 0),
+        ("z", 5, 3, 0), ("z", 6, 1, 0), ("z", 9, 1, 0), ("z", 7, 2, 0), ("z", 10, 1, 0),
+        ("z", 8, 1, 0), ("kvw",), ("z", 5, 4, 0), ("z", 4, 4, 0), ("y", 2), ("z", 6, 2, 0),
+        ("y", 1), ("y", 3), ("z", 8, 1, 1),
     ), ("K", 0)),
     ((
-        ("own", 10), ("z", 6, 3, 0), ("yf", 8), ("z", 8, 2, 0), ("y", 3), ("kvw",),
+        ("z", 7, 3, 0), ("z", 9, 2, 0), ("z", 10, 2, 0),
     ), ("P", 0)),
     ((
-        ("z", 7, 3, 0), ("z", 5, 4, 0), ("z", 9, 2, 0),
+        ("z", 6, 3, 0), ("b1",), ("z", 8, 2, 0),
     ), ("A", 0)),
     ((
-        ("z", 10, 1, 0),
+        ("z", 8, 2, 1), ("y", 4), ("z", 7, 4, 0), ("y", 5), ("z", 9, 3, 0),
+    ), ("K", 1)),
+    ((
+        ("z", 6, 4, 0), ("z", 10, 3, 0), ("z", 8, 3, 0), ("b2",),
+    ), ("P", 3)),
+    ((
+        ("z", 8, 3, 1), ("z", 9, 4, 0),
+    ), ("A", 3)),
+    ((
+        ("z", 10, 4, 0), ("y", 7), ("y", 6),
+    ), ("P", 1)),
+    ((
+
     ), ("A", 1)),
     ((
-        ("z", 6, 4, 0), ("z", 8, 1, 1), ("z", 8, 3, 0), ("z", 7, 4, 0), ("b1",), ("z", 9, 3, 0),
-        ("z", 10, 2, 0), ("y", 4), ("y", 5),
-    ), ("K", 1)),
-    ((
-        ("z", 8, 2, 1), ("z", 8, 4, 0), ("z", 9, 4, 0), ("y", 6), ("y", 7),
-    ), ("P", 1)),
-    ((
-        ("z", 10, 3, 0),
+        ("y", 9), ("z", 8, 4, 1), ("z", 8, 4, 0), ("y", 8),
+    ), ("P", 2)),
+    ((
+
     ), ("A", 2)),
-    ((
-
-    ), ("A", 3)),
-    ((
-        ("z", 8, 3, 1), ("b2",),
-    ), ("P", 3)),
-    ((
-        ("z", 10, 4, 0),
-    ), ("A", 6)),
-    ((
-
-    ), ("A", 7)),
-    ((
-        ("z", 8, 4, 1), ("y", 8), ("y", 9),
-    ), ("P", 2)),
-    ((
-
-    ), ("A", 4)),
-    ((
-
-    ), ("A", 5)),
     ((
         ("y", 10), ("b3",),
     ), ("P", 4)),
     ((
 
-    ), ("A", 8)),
-    ((
-
-    ), ("A", 9)),
+    ), ("A", 4)),
 )
-AHEAD = sum(op[0] == "own" for op in SCHEDULE[0][0])
+AHEAD = [op[0] == "own" for op in SCHEDULE[0][0] + (("",),)].index(False)
 
 
 def angle_tables(head_dim):
@@ -196,6 +181,10 @@
     def slot_of(i):
         return 10 + x if i == 0 else PLACE[i]
 
+    barrier = pltpu.get_barrier_semaphore()
+    for device in (partner, xp, xm, yp, ym, zp, zm):
+        pl.semaphore_signal(barrier, inc=1, device_id=device, device_id_type=MESH)
+
     tok_load = pltpu.make_async_copy(tok_ref, tokbuf.at[0], misc_sem.at[0])
     loads = []
     for i in range(CHUNKS):
@@ -232,9 +221,6 @@
     for copy in kv_loads + loads[:AHEAD] + [tok_load] + flat_loads + [table_load, list_load] + loads[AHEAD:]:
         copy.start()
 
-    barrier = pltpu.get_barrier_semaphore()
-    for device in (partner, xp, xm, yp, ym, zp, zm):
-        pl.semaphore_signal(barrier, inc=1, device_id=device, device_id_type=MESH)
     pl.semaphore_wait(barrier, 7)
 
     shard_rows = wbuf.shape[2]
@@ -242,7 +228,7 @@
 
     def send_y(i, slot, shard, distance):
         row = y_lo * NZ + shard
-        cut = half - 16 if distance <= 1 else half
+        cut = half - 16 if distance <= NEAR else half
         lower, upper = wbuf.at[slot, row, 0:cut], wbuf.at[slot, row, cut:shard_rows]
         remote(lower, lower, y_send.at[i], y_recv.at[i], ykv).start()
         remote(upper, upper, y_send.at[i], y_recv.at[i], yother).start()
@@ -310,21 +296,24 @@
             )
         )
 
-    def pair(at_x, at_y):
-        return kvbuf.at[pl.ds(at_x * 4 + at_y * 2, 2)]
+    def cached(at_x, at_y, side):
+        return kvbuf.at[at_x * 4 + at_y * 2 + (core if side == 0 else 1 - core)]
 
     left_x, right_x, far_x = (x + 3) % NX, (x + 1) % NX, (x + 2) % NX
-    kv_y = remote(pair(x, y_hi), pair(x, y_hi), kv_send.at[1], kv_recv.at[1], ykv)
-    kv_x = [
-        remote(pair(x, y_hi), pair(x, y_hi), kv_send.at[2], kv_recv.at[2], xp),
-        remote(pair(x, y_hi), pair(x, y_hi), kv_send.at[3], kv_recv.at[3], xm),
-        remote(pair(x, 1 - y_hi), pair(x, 1 - y_hi), kv_send.at[4], kv_recv.at[4], xp),
-        remote(pair(x, 1 - y_hi), pair(x, 1 - y_hi), kv_send.at[5], kv_recv.at[5], xm),
-        remote(pair(left_x, y_hi), pair(left_x, y_hi), kv_send.at[6], kv_recv.at[6], xp),
-        remote(
-            pair(right_x, 1 - y_hi), pair(right_x, 1 - y_hi), kv_send.at[7], kv_recv.at[7], xm
-        ),
-    ]
+
+    def kv_copy(number, side):
+        at_x, at_y, device = (
+            (x, y_hi, ykv),
+            (x, y_hi, xp),
+            (x, y_hi, xm),
+            (x, 1 - y_hi, xp),
+            (x, 1 - y_hi, xm),
+            (left_x, y_hi, xp),
+            (right_x, 1 - y_hi, xm),
+        )[number]
+        block = cached(at_x, at_y, side)
+        number = 1 + 7 * side + number
+        return remote(block, block, kv_send.at[number], kv_recv.at[number], device)
 
     def shared(at_x, upper):
         return wbuf.at[10 + at_x, 8:16] if upper else wbuf.at[10 + at_x, 0:8]
@@ -405,22 +394,23 @@
     column_at = lax.broadcasted_iota(jnp.int32, (QBLK, QBLK), 1)
     blocks = rows // QBLK
 
-    def attend(n, slot):
-        local = slot % 10
-        head = local // GROUP
-        scores, values = [], []
-        for block in range(2 * blocks):
+    def attend(slots):
+        todo = [(n, block) for n in range(2) for block in range(2 * blocks)]
+        scores, values = {}, {}
+        for n, block in todo:
+            local = slots[n] % 10
+            head = local // GROUP
             at = slice(block * QBLK, (block + 1) * QBLK)
             keys, shifts = [], []
-            values.append([])
+            values[n, block] = []
             for step in range(SEL):
                 index = lsmem[block // blocks, block % blocks, step, core * 10 + local]
                 shifts.append(jnp.where(index >= 0, 0.0, -jnp.inf))
                 index = jnp.maximum(index, 0)
                 keys.append(kvbuf[index, head])
-                values[-1].append(kvbuf[index, 2 + head])
+                values[n, block].append(kvbuf[index, 2 + head])
             keys.append(knew[head, at, :])
-            values[-1].append(vnew[head, at, :])
+            values[n, block].append(vnew[head, at, :])
             all_keys = lax.dot_general(
                 qbuf[n, at, :],
                 jnp.concatenate(keys, axis=0),
@@ -431,27 +421,28 @@
                 all_keys[:, step * QBLK : (step + 1) * QBLK] + shifts[step] for step in range(SEL)
             ]
             near = all_keys[:, SEL * QBLK :]
-            scores.append(parts + [jnp.where(row_at >= column_at, near, -jnp.inf)])
-        largest = [
-            jnp.max(functools.reduce(jnp.maximum, parts), axis=1, keepdims=True)
-            for parts in scores
-        ]
-        for block in list(range(blocks, 2 * blocks)) + list(range(blocks)):
-            weights = [jnp.exp2(part - largest[block]) for part in scores[block]]
+            scores[n, block] = parts + [jnp.where(row_at >= column_at, near, -jnp.inf)]
+        largest = {
+            at: jnp.max(functools.reduce(jnp.maximum, scores[at]), axis=1, keepdims=True)
+            for at in todo
+        }
+        for n, block in sorted(todo, key=lambda at: (at[1] < blocks, at)):
+            weights = [jnp.exp2(part - largest[n, block]) for part in scores[n, block]]
             total = jnp.sum(functools.reduce(jnp.add, weights), axis=1, keepdims=True)
             mixed = jnp.dot(
                 jnp.concatenate([part.astype(jnp.bfloat16) for part in weights], axis=1),
-                jnp.concatenate(values[block], axis=0),
+                jnp.concatenate(values[n, block], axis=0),
                 preferred_element_type=jnp.float32,
             )
             result = mixed * (1.0 / total)
+            place = core * 10 + slots[n] % 10
             at = slice(block % blocks * QBLK, (block % blocks + 1) * QBLK)
             if block >= blocks:
-                ostage[slot, at, :] = result
+                ostage[slots[n], at, :] = result
             else:
-                out_ref[core * 10 + local, at, :] = result
+                out_ref[place, at, :] = result
             if block == 2 * blocks - 1:
-                copy_out(slot, core * 10 + local)
+                copy_out(slots[n], place)
 
     def query_chunks(first, second):
         heads = (core * 10 + first % 10, core * 10 + second % 10)
@@ -462,7 +453,8 @@
     tok_send = remote(tok_ref, tokbuf.at[1], misc_send.at[0], misc_sem.at[1], partner)
     list_send = remote(lists_ref, lvmem, misc_send.at[1], misc_sem.at[2], partner)
 
-    def kv_wait(landed, number):
+    def kv_wait(landed, number, side):
+        number = 1 + 7 * side + number
         remote(landed, landed, kv_send.at[number], kv_recv.at[number], xp).wait_recv()
 
     def shared_wait(landed, number):
@@ -479,27 +471,30 @@
         elif kind == "y":
             wait_y(*at)
         elif kind == "kv0":
-            for copy in kv_loads:
-                copy.wait()
-            kv_wait(kvbuf.at[ctx + 1 - 2 * core], 0)
-            kv_y.start()
-            kv_x[0].start()
-            kv_x[1].start()
+            if at[0] == 0:
+                for copy in kv_loads:
+                    copy.wait()
+            else:
+                other = kvbuf.at[ctx + 1 - 2 * core]
+                remote(other, other, kv_send.at[0], kv_recv.at[0], partner).wait_recv()
+            for number in range(3):
+                kv_copy(number, at[0]).start()
         elif kind == "kv1":
-            kv_wait(pair(x, 1 - y_hi), 1)
-            kv_x[2].start()
-            kv_x[3].start()
+            kv_wait(cached(x, 1 - y_hi, at[0]), 0, at[0])
+            kv_copy(3, at[0]).start()
+            kv_copy(4, at[0]).start()
         elif kind == "kv2":
-            kv_wait(pair(left_x, y_hi), 2)
-            kv_x[4].start()
+            kv_wait(cached(left_x, y_hi, at[0]), 1, at[0])
+            kv_copy(5, at[0]).start()
         elif kind == "kv3":
-            kv_wait(pair(right_x, 1 - y_hi), 5)
-            kv_x[5].start()
+            kv_wait(cached(right_x, 1 - y_hi, at[0]), 4, at[0])
+            kv_copy(6, at[0]).start()
         elif kind == "kvw":
-            kv_wait(pair(right_x, y_hi), 3)
-            kv_wait(pair(left_x, 1 - y_hi), 4)
-            kv_wait(pair(far_x, y_hi), 6)
-            kv_wait(pair(far_x, 1 - y_hi), 7)
+            for side in range(2):
+                kv_wait(cached(right_x, y_hi, side), 2, side)
+                kv_wait(cached(left_x, 1 - y_hi, side), 3, side)
+                kv_wait(cached(far_x, y_hi, side), 5, side)
+                kv_wait(cached(far_x, 1 - y_hi, side), 6, side)
         elif kind == "b0":
             wait_y(0)
             for copy in x_copies[:4]:
@@ -599,12 +594,16 @@
                 pick_query([second for _, second in pairs]),
             )
 
-        condition, pick_head = on("A")
+        condition, pick_heads = on("A")
 
         @pl.when(condition)
         def _():
-            flat = [slot for both in pairs for slot in both]
-            attend(pick_head([n % 2 for n in range(len(flat))]), pick_head(flat))
+            attend(
+                (
+                    pick_heads([first for first, _ in pairs]),
+                    pick_heads([second for _, second in pairs]),
+                )
+            )
 
     for i in range(CHUNKS):
         sent = wbuf.at[0, 0:14] if i in Y_FIRST else wbuf.at[0, 0:7]
@@ -615,9 +614,9 @@
     for copy in x_copies:
         copy.wait_send()
     pltpu.make_async_copy(kvbuf.at[0], kvbuf.at[0], kv_send.at[0]).wait()
-    kv_y.wait_send()
-    for copy in kv_x:
-        copy.wait_send()
+    for side in range(2):
+        for number in range(7):
+            kv_copy(number, side).wait_send()
     tok_send.wait_send()
     list_send.wait_send()
     written = ostage
@@ -699,8 +698,8 @@
             dma((6,)),
             dma((6,)),
             dma((4,)),
-            dma((8,)),
-            dma((8,)),
+            dma((15,)),
+            dma((15,)),
             dma((10,)),
             dma((2,)),
             dma((1,)),

time: 69.2 us -> 63.7 us (0.921)
  Pallas kernels: 67.8 us -> 62.3 us
    pallas_call x1, Pallas kernels: 65.8 us -> 60.2 us  [on_device(): pl.pallas_call(kernel, out_shape=pltpu.VMEM((28, rows, HD), jnp.float32),...]
where the time goes in v4:
time: 63.7 us; the launch traced here: 63.6 us
  Pallas kernels  62.3 us (98%)
  between operations  1.29 us (2%)
    pallas_call x1, Pallas kernels, on_device(): pl.pallas_call(kernel, out_shape=pltpu.VMEM((28, rows, HD), jnp.float32),...  60.2 us
    pallas_call x1, Pallas kernels, on_device(): pl.pallas_call(write_kernel, out_shape=(jax.ShapeDtypeStruct((rows, 20 *...  2.06 us

profile of v4, /device:TPU:1, one launch (start us, length us, event | category | flops | bytes accessed | tf_op | source)
XLA Modules:
  0.0 63.6 jit_solution(12382935630060468211)
XLA Ops:
  1.3 60.2 %gather_attend.1.source = f32[28,256,128]{2,1,0:T(8,128)S(1)} custom-call(s32[1]{0:T(128)S(6)} %copy.16.start_ref, bf16[256,2560]{1,0:T(8,128)(2,1)} %tok_ref.1, bf16[160,2560]{1,0:T(8,128)(2,1)} %wq_ref.1, bf16[160,512]{1,0:T(8,128)(2,1)} %wk_ref.1, bf16[160,512]{1,0:T(8,128)(2,1)} %wv_ref.1, bf16[128,512]{1,0:T(8,128)(2,1)} %ck_ref.1, ...), custom_call_target="tpu_custom_call" | custom-call | tf_op jit(solution)/shard_map/gather_attend/pallas_call | solution.py:667
  61.5 2.1 %write_out.1 = (f32[256,2560]{1,0:T(8,128)}, f32[256,512]{1,0:T(8,128)}, f32[256,512]{1,0:T(8,128)}) custom-call(f32[28,256,128]{2,1,0:T(8,128)S(1)} %gather_attend.1.source), custom_call_target="tpu_custom_call" | custom-call | tf_op jit(solution)/shard_map/write_out/pallas_call | solution.py:727

commit v5 on v4

--- a/solution.py
+++ b/solution.py
@@ -27,47 +27,47 @@
 NEAR = 1
 SCHEDULE = (
     ((
-        ("own", 0), ("own", 3), ("kv0", 0), ("own", 1), ("own", 5), ("own", 2), ("kv0", 1),
-        ("z", 0, 1, 0), ("z", 3, 1, 0),
+        ("own", 0), ("own", 1), ("own", 3), ("own", 4), ("own", 2), ("kv0", 0), ("kv0", 1),
     ), ("N0",)),
     ((
-        ("own", 4), ("z", 5, 1, 0), ("z", 1, 1, 0), ("kv1", 0),
+        ("z", 0, 1, 0), ("own", 5), ("z", 3, 1, 0), ("z", 1, 1, 0), ("z", 4, 1, 0),
+        ("z", 0, 2, 0), ("kv1", 0), ("z", 2, 1, 0), ("own", 8), ("own", 9),
     ), ("T",)),
     ((
-        ("z", 0, 2, 0), ("z", 2, 1, 0), ("z", 3, 2, 0), ("kv2", 0), ("z", 4, 1, 0), ("kv1", 1),
-        ("z", 1, 2, 0), ("z", 0, 3, 0), ("own", 7), ("own", 6), ("z", 2, 2, 0), ("own", 8),
-        ("kv3", 0), ("kv2", 1), ("z", 0, 4, 0), ("z", 4, 2, 0), ("z", 3, 3, 0), ("kv3", 1),
-        ("z", 5, 2, 0), ("z", 1, 3, 0), ("z", 2, 3, 0), ("z", 7, 1, 0), ("b0",), ("own", 9),
+        ("kv2", 0), ("kv1", 1), ("z", 1, 2, 0), ("z", 0, 3, 0), ("z", 5, 1, 0), ("z", 2, 2, 0),
+        ("own", 6),
     ), ("N1",)),
     ((
-        ("yf", 8), ("own", 10), ("z", 3, 4, 0), ("z", 2, 4, 0), ("z", 4, 3, 0), ("z", 1, 4, 0),
-        ("z", 5, 3, 0), ("z", 6, 1, 0), ("z", 9, 1, 0), ("z", 7, 2, 0), ("z", 10, 1, 0),
-        ("z", 8, 1, 0), ("kvw",), ("z", 5, 4, 0), ("z", 4, 4, 0), ("y", 2), ("z", 6, 2, 0),
-        ("y", 1), ("y", 3), ("z", 8, 1, 1),
+        ("kv3", 0), ("kv2", 1), ("own", 7), ("z", 0, 4, 0), ("z", 3, 2, 0), ("kv3", 1),
+        ("z", 1, 3, 0), ("z", 4, 2, 0), ("z", 2, 3, 0), ("z", 6, 1, 0), ("z", 7, 1, 0), ("b0",),
+        ("z", 3, 3, 0), ("z", 5, 2, 0), ("z", 1, 4, 0), ("yf", 8), ("z", 2, 4, 0), ("own", 10),
+        ("z", 4, 3, 0), ("z", 6, 2, 0), ("z", 3, 4, 0), ("z", 7, 2, 0), ("z", 5, 3, 0),
+        ("z", 9, 1, 0), ("kvw",), ("z", 8, 1, 0), ("z", 4, 4, 0), ("y", 1), ("z", 10, 1, 0),
+        ("y", 2), ("z", 8, 1, 1),
     ), ("K", 0)),
     ((
-        ("z", 7, 3, 0), ("z", 9, 2, 0), ("z", 10, 2, 0),
+        ("z", 5, 4, 0), ("z", 6, 3, 0), ("z", 7, 3, 0), ("z", 9, 2, 0), ("y", 3),
     ), ("P", 0)),
     ((
-        ("z", 6, 3, 0), ("b1",), ("z", 8, 2, 0),
+        ("z", 10, 2, 0), ("z", 8, 2, 0), ("b1",), ("z", 8, 2, 1),
     ), ("A", 0)),
     ((
-        ("z", 8, 2, 1), ("y", 4), ("z", 7, 4, 0), ("y", 5), ("z", 9, 3, 0),
+        ("y", 4), ("z", 7, 4, 0), ("z", 6, 4, 0), ("z", 9, 3, 0), ("y", 5),
     ), ("K", 1)),
     ((
-        ("z", 6, 4, 0), ("z", 10, 3, 0), ("z", 8, 3, 0), ("b2",),
+        ("z", 10, 3, 0), ("b2",),
     ), ("P", 3)),
     ((
-        ("z", 8, 3, 1), ("z", 9, 4, 0),
+        ("z", 8, 3, 0), ("z", 8, 3, 1), ("z", 9, 4, 0),
     ), ("A", 3)),
     ((
-        ("z", 10, 4, 0), ("y", 7), ("y", 6),
+        ("y", 7), ("y", 6),
     ), ("P", 1)),
     ((
-
+        ("z", 10, 4, 0),
     ), ("A", 1)),
     ((
-        ("y", 9), ("z", 8, 4, 1), ("z", 8, 4, 0), ("y", 8),
+        ("z", 8, 4, 1), ("z", 8, 4, 0), ("y", 9), ("y", 8),
     ), ("P", 2)),
     ((
 
@@ -371,7 +371,7 @@
         return linear * cosine[...] + pltpu.roll(linear, HD // 2, 1) * sine[...]
 
     def copy_out(slot, place):
-        other, target = ostage.at[slot], out_ref.at[place]
+        other, target = ostage.at[slot], out_ref.at[:, columns(place)]
         remote(other, target, out_send.at[0], out_recv.at[0], partner).start()
 
     def key_value_chunks(head):
@@ -383,11 +383,11 @@
         knew[head] = key.astype(jnp.bfloat16)
         ostage[2 * head] = key[rows:]
         copy_out(2 * head, 20 + global_head)
-        out_ref[20 + global_head] = key[:rows]
+        out_ref[:, columns(20 + global_head)] = key[:rows]
         vnew[head] = linear_value.astype(jnp.bfloat16)
         ostage[2 * head + 1] = linear_value[rows:]
         copy_out(2 * head + 1, 24 + global_head)
-        out_ref[24 + global_head] = linear_value[:rows]
+        out_ref[:, columns(24 + global_head)] = linear_value[:rows]
 
     scale = HD**-0.5 * math.log2(math.e)
     row_at = lax.broadcasted_iota(jnp.int32, (QBLK, QBLK), 0)
@@ -440,7 +440,7 @@
             if block >= blocks:
                 ostage[slots[n], at, :] = result
             else:
-                out_ref[place, at, :] = result
+                out_ref[at, columns(place)] = result
             if block == 2 * blocks - 1:
                 copy_out(slots[n], place)
 
@@ -626,16 +626,16 @@
 
 def write_kernel(source, ctx_ref, keys_ref, values_ref, sem):
     copies = []
-    for place in range(28):
-        target, first = ((ctx_ref, 0), (keys_ref, 20), (values_ref, 24))[
-            (place >= 20) + (place >= 24)
-        ]
-        column = (place - first) * HD
-        copies.append(
-            pltpu.make_async_copy(
-                source.at[place], target.at[:, column : column + HD], sem.at[place]
-            )
-        )
+    rows = source.shape[0] // 4
+    for part in range(4):
+        at = slice(part * rows, (part + 1) * rows)
+        for n, (target, first) in enumerate(((ctx_ref, 0), (keys_ref, 20), (values_ref, 24))):
+            column = slice(first * HD, first * HD + target.shape[1])
+            copies.append(
+                pltpu.make_async_copy(
+                    source.at[at, column], target.at[at, :], sem.at[part * 3 + n]
+                )
+            )
     for copy in copies:
         copy.start()
     for copy in copies:
@@ -666,7 +666,7 @@
     dma = pltpu.SemaphoreType.DMA
     heads_out = pl.pallas_call(
         kernel,
-        out_shape=pltpu.VMEM((28, rows, HD), jnp.float32),
+        out_shape=pltpu.VMEM((rows, 28 * HD), jnp.float32),
         in_specs=[smem] + [hbm] * 12,
         out_specs=pl.BlockSpec(memory_space=pltpu.VMEM),
         scratch_shapes=[
@@ -733,7 +733,7 @@
         ),
         in_specs=[vmem],
         out_specs=[hbm] * 3,
-        scratch_shapes=[dma((28,))],
+        scratch_shapes=[dma((12,))],
         compiler_params=pltpu.CompilerParams(vmem_limit_bytes=4 << 20),
         name="write_out",
     )(heads_out)

time: 63.7 us -> 63.3 us (level)
  no operation moved by 1% of the time
where the time goes in v5:
time: 63.3 us; the launch traced here: 63.2 us
  Pallas kernels  61.9 us (98%)
  between operations  1.29 us (2%)
    pallas_call x1, Pallas kernels, on_device(): pl.pallas_call(kernel, out_shape=pltpu.VMEM((rows, 28 * HD), jnp.float32)...  59.9 us
    pallas_call x1, Pallas kernels, on_device(): pl.pallas_call(write_kernel, out_shape=(jax.ShapeDtypeStruct((rows, 20 *...  1.93 us

profile of v5, /device:TPU:1, one launch (start us, length us, event | category | flops | bytes accessed | tf_op | source)
XLA Modules:
  0.0 63.2 jit_solution(5856023419831269537)
XLA Ops:
  1.3 59.9 %gather_attend.1.source = f32[256,3584]{1,0:T(8,128)S(1)} custom-call(s32[1]{0:T(128)S(6)} %copy.16.start_ref, bf16[256,2560]{1,0:T(8,128)(2,1)} %tok_ref.1, bf16[160,2560]{1,0:T(8,128)(2,1)} %wq_ref.1, bf16[160,512]{1,0:T(8,128)(2,1)} %wk_ref.1, bf16[160,512]{1,0:T(8,128)(2,1)} %wv_ref.1, bf16[128,512]{1,0:T(8,128)(2,1)} %ck_ref.1, ...), custom_call_target="tpu_custom_call" | custom-call | tf_op jit(solution)/shard_map/gather_attend/pallas_call | solution.py:667
  61.2 1.9 %write_out.1 = (f32[256,2560]{1,0:T(8,128)}, f32[256,512]{1,0:T(8,128)}, f32[256,512]{1,0:T(8,128)}) custom-call(f32[256,3584]{1,0:T(8,128)S(1)} %gather_attend.1.source), custom_call_target="tpu_custom_call" | custom-call | tf_op jit(solution)/shard_map/write_out/pallas_call | solution.py:727

commit v6 on v5

--- a/solution.py
+++ b/solution.py
@@ -58,11 +58,8 @@
         ("z", 10, 3, 0), ("b2",),
     ), ("P", 3)),
     ((
-        ("z", 8, 3, 0), ("z", 8, 3, 1), ("z", 9, 4, 0),
-    ), ("A", 3)),
-    ((
-        ("y", 7), ("y", 6),
-    ), ("P", 1)),
+        ("z", 8, 3, 0), ("z", 8, 3, 1), ("z", 9, 4, 0), ("y", 7), ("y", 6),
+    ), ("X", 0)),
     ((
         ("z", 10, 4, 0),
     ), ("A", 1)),
@@ -394,7 +391,7 @@
     column_at = lax.broadcasted_iota(jnp.int32, (QBLK, QBLK), 1)
     blocks = rows // QBLK
 
-    def attend(slots):
+    def attend(slots, base):
         todo = [(n, block) for n in range(2) for block in range(2 * blocks)]
         scores, values = {}, {}
         for n, block in todo:
@@ -412,7 +409,7 @@
             keys.append(knew[head, at, :])
             values[n, block].append(vnew[head, at, :])
             all_keys = lax.dot_general(
-                qbuf[n, at, :],
+                qbuf[base + n, at, :],
                 jnp.concatenate(keys, axis=0),
                 (((1,), (1,)), ((), ())),
                 preferred_element_type=jnp.float32,
@@ -444,11 +441,11 @@
             if block == 2 * blocks - 1:
                 copy_out(slots[n], place)
 
-    def query_chunks(first, second):
+    def query_chunks(first, second, base):
         heads = (core * 10 + first % 10, core * 10 + second % 10)
         linear = project((first, second), heads)
         for n in range(2):
-            qbuf[n] = (rope(linear[n]) * scale).astype(jnp.bfloat16)
+            qbuf[base + n] = (rope(linear[n]) * scale).astype(jnp.bfloat16)
 
     tok_send = remote(tok_ref, tokbuf.at[1], misc_send.at[0], misc_sem.at[1], partner)
     list_send = remote(lists_ref, lvmem, misc_send.at[1], misc_sem.at[2], partner)
@@ -592,7 +589,13 @@
             query_chunks(
                 pick_query([first for first, _ in pairs]),
                 pick_query([second for _, second in pairs]),
-            )
+                0,
+            )
+
+        @pl.when(on("X")[0])
+        def _():
+            query_chunks(*pairs[1], 2)
+            attend(pairs[3], 0)
 
         condition, pick_heads = on("A")
 
@@ -602,7 +605,8 @@
                 (
                     pick_heads([first for first, _ in pairs]),
                     pick_heads([second for _, second in pairs]),
-                )
+                ),
+                pick_heads((0, 2, 0, 0, 0)),
             )
 
     for i in range(CHUNKS):
@@ -676,7 +680,7 @@
             pltpu.VMEM((2 * rows, features), jnp.bfloat16),
             pltpu.VMEM((2 * rows, HD), jnp.float32),
             pltpu.VMEM((2 * rows, HD), jnp.float32),
-            pltpu.VMEM((2, 2 * rows, HD), jnp.bfloat16),
+            pltpu.VMEM((4, 2 * rows, HD), jnp.bfloat16),
             pltpu.VMEM((2, 2 * rows, HD), jnp.bfloat16),
             pltpu.VMEM((2, 2 * rows, HD), jnp.bfloat16),
             pltpu.VMEM((14, rows, HD), jnp.float32),

time: 63.3 us -> 63.7 us (level)
  no operation moved by 1% of the time
where the time goes in v6:
time: 63.7 us; the launch traced here: 63.6 us
  Pallas kernels  62.3 us (98%)
  between operations  1.29 us (2%)
    pallas_call x1, Pallas kernels, on_device(): pl.pallas_call(kernel, out_shape=pltpu.VMEM((rows, 28 * HD), jnp.float32)...  60.4 us
    pallas_call x1, Pallas kernels, on_device(): pl.pallas_call(write_kernel, out_shape=(jax.ShapeDtypeStruct((rows, 20 *...  1.93 us

profile of v6, /device:TPU:1, one launch (start us, length us, event | category | flops | bytes accessed | tf_op | source)
XLA Modules:
  0.0 63.6 jit_solution(18416220525784078965)
XLA Ops:
  1.3 60.4 %gather_attend.1.source = f32[256,3584]{1,0:T(8,128)S(1)} custom-call(s32[1]{0:T(128)S(6)} %copy.16.start_ref, bf16[256,2560]{1,0:T(8,128)(2,1)} %tok_ref.1, bf16[160,2560]{1,0:T(8,128)(2,1)} %wq_ref.1, bf16[160,512]{1,0:T(8,128)(2,1)} %wk_ref.1, bf16[160,512]{1,0:T(8,128)(2,1)} %wv_ref.1, bf16[128,512]{1,0:T(8,128)(2,1)} %ck_ref.1, ...), custom_call_target="tpu_custom_call" | custom-call | tf_op jit(solution)/shard_map/gather_attend/pallas_call | solution.py:671
  61.7 1.9 %write_out.1 = (f32[256,2560]{1,0:T(8,128)}, f32[256,512]{1,0:T(8,128)}, f32[256,512]{1,0:T(8,128)}) custom-call(f32[256,3584]{1,0:T(8,128)S(1)} %gather_attend.1.source), custom_call_target="tpu_custom_call" | custom-call | tf_op jit(solution)/shard_map/write_out/pallas_call | solution.py:731
